TPU v7x, 32 devices: a whole 2x2x4 slice. The times are simulated.
32 devices in a mesh: oct: 2 (over x), space: 16 (over z, y, core).
Axes of the slice: x: 2, y: 2, z: 4, core: 2. Of those that a mesh axis runs over, the one named last changes fastest.
Arguments:
- distribution: float32 [1000, 96, 128], P('oct', 'space'), may hold values from 0.05 to 1
- collision_scale: float32 [1, 96, 128], P(None, 'space'), may hold values from 0.4 to 2.5
Outputs:
- advanced: float32 [1000, 96, 128], P('oct', 'space')
All inputs are finite; a program needn't handle non-finite values.
Results may differ from a plain program's by a relative error of at most 0.0003.
Values sent between devices are 32-bit elements; how exact they have to be, the bound alone decides.
No kernel may reach another device: no remote copies, remote signals or barrier semaphores. Data moves between devices by JAX's collectives and lax.ppermute only.
A program may use at most 64 MiB of HBM per device.

v0:
```python
import functools
import math

import jax
import jax.numpy as jnp
import numpy as np
from jax import lax
from jax.experimental import pallas as pl
from jax.experimental.pallas import tpu as pltpu
from jax.sharding import PartitionSpec as P

NV = 10
NZ = 16
NY = 8
HALF = NV // 2
PER = HALF**3
LANES = 128

vel_bound = 4.0
courant = 0.08
time_step = 0.08
base_rate = 0.25
visc_index = 0.81
limiter_eps = 0.01
spacing = 2.0 * vel_bound / NV
quad = spacing**3 * (2.0 * math.pi) ** (-1.5)
unit = 0.5 * spacing
log2e = math.log2(math.e)

VMEM = pl.BlockSpec(memory_space=pltpu.VMEM)
SMEM = pl.BlockSpec(memory_space=pltpu.SMEM)
NT = (((1,), (1,)), ((), ()))
TN = (((0,), (0,)), ((), ()))
F32 = jnp.float32
BF16 = jnp.bfloat16


def tables():
    within = np.arange(PER)
    size = np.stack([within // HALF**2, within // HALF % HALF, within % HALF]) * 2 + 1
    feature = np.zeros((8, 8, LANES), np.float32)
    half = np.zeros((8, 8, LANES), np.float32)
    for octant in range(8):
        sign = np.array([1 - 2 * (octant >> 2 & 1), 1 - 2 * (octant >> 1 & 1), 1 - 2 * (octant & 1)])
        feature[octant, 0, :PER] = 1
        feature[octant, 1:4, :PER] = size * sign[:, None]
        feature[octant, 4, :PER] = (size * size).sum(0)
        half[octant, :3, :PER] = 0.5 * courant * unit * size
    pad = np.zeros_like(feature)
    phi = np.concatenate([feature, feature, feature, pad], axis=1)
    weight = np.concatenate([feature, pad], axis=1)
    keep = np.zeros((32, LANES), np.float32)
    keep[[5, 13, 21]] = 1
    return (
        jnp.asarray(phi, BF16),
        jnp.asarray(keep, BF16),
        jnp.asarray(weight, BF16),
        jnp.asarray(half, F32),
    )


def slope(left, right, left_sq, right_sq):
    return (left * right) * (left + right) * (1.0 / (left_sq + right_sq))


def place_octant(octant):
    pos_y = octant // 2 % 2 == 0
    pos_z = octant % 2 == 0
    roll_y = jnp.where(pos_y, 1, NY - 1)
    first = jnp.where(pos_z, 0, (NZ - 1) * NY)
    pace = jnp.where(pos_z, NY, -NY)
    offs = [pl.multiple_of(first + i * pace, NY) for i in range(NZ)]
    return roll_y, offs


def convert(load, store, tmp, octants):
    for o in range(octants):
        x = load(o)
        x = jnp.concatenate([x, jnp.zeros((LANES - PER, LANES), F32)], 0)
        tmp[o] = x.T
        for z in range(NZ):
            store(o, z, tmp[o, pl.ds(z, NY, stride=NZ), :])


def coefficients(total, scale):
    m0 = total[0:1]
    inv = 1.0 / m0
    ux = unit * total[1:2] * inv
    uy = unit * total[2:3] * inv
    uz = unit * total[3:4] * inv
    square = ux * ux + uy * uy + uz * uz
    temper = (unit * unit * total[4:5] * inv - square) * (1.0 / 3.0)
    log_t = jnp.log2(temper)
    density = quad * m0
    pace = (time_step * base_rate) * scale * density
    keep = 1.0 - pace * jnp.exp2((1.0 - visc_index) * log_t)
    beta = log2e / temper
    c0 = jnp.log2(pace * density) + (1.0 - visc_index - 1.5) * log_t - 0.5 * beta * square
    slow = unit * beta
    row = lax.broadcasted_iota(jnp.int32, (8, LANES), 0)
    c = jnp.where(row == 0, c0, 0.0)
    c = jnp.where(row == 1, slow * ux, c)
    c = jnp.where(row == 2, slow * uy, c)
    c = jnp.where(row == 3, slow * uz, c)
    c = jnp.where(row == 4, (-0.5 * unit) * slow, c)
    c = jnp.where(row == 5, keep, c)
    high = c.astype(BF16).astype(F32)
    rest = c - high
    middle = rest.astype(BF16).astype(F32)
    low = rest - middle
    return jnp.concatenate([high, middle, low, jnp.zeros_like(c)], 0).astype(BF16)


def moments_of(x, weight):
    high = x.astype(BF16)
    low = (x - high.astype(F32)).astype(BF16)
    m = lax.dot_general(weight, high, NT, preferred_element_type=F32)
    m = m + lax.dot_general(weight, low, NT, preferred_element_type=F32)
    return m[:8]


def prepare(js, coef, tabs, keep_ref):
    for n, j in enumerate(js):
        keep_ref[n] = lax.dot_general(coef[j], tabs[1][...], TN, preferred_element_type=F32)


def advance(js, get, o, octant, place, coef, tabs, arg, keep_ref, carry, emit):
    roll_y, offs = place
    back_y = NY - roll_y
    half = tabs[3][octant]
    hx, hy, hz = half[0:1], half[1:2], half[2:3]
    for n, j in enumerate(js):
        arg[n] = lax.dot_general(coef[j], tabs[0][octant], TN, preferred_element_type=F32)

    def rd(j, i):
        ref, index = get(j)
        return ref[index, o, pl.ds(offs[i % NZ], NY), :]

    eps2 = 0.5 * limiter_eps
    j = js[0] - 1
    for i in range(NZ):
        x = rd(j, i)
        a = x - rd(j - 1, i)
        b = rd(j + 1, i) - x
        bb = b * b + eps2
        s = pl.ds(i * NY, NY)
        carry[0, s, :] = (x + x) + slope(a, b, a * a + eps2, bb)
        carry[1, s, :] = b
        carry[2, s, :] = bb
    for n, j in enumerate(js):
        xm2, xm1, x0 = rd(j, NZ - 2), rd(j, NZ - 1), rd(j, 0)
        am, az = xm1 - xm2, x0 - xm1
        ez = az * az + eps2
        gz = (xm1 + xm1) + slope(am, az, am * am + eps2, ez)
        for i in range(NZ):
            s = pl.ds(i * NY, NY)
            x, xn = x0, rd(j, i + 1)
            x2 = x + x
            an = xn - x
            en = an * an + eps2
            gn = x2 + slope(az, an, ez, en)
            acc = hz * (gn - gz)
            az, ez, gz, x0 = an, en, gn, xn
            b = rd(j + 1, i) - x
            bb = b * b + eps2
            g = x2 + slope(carry[1, s, :], b, carry[2, s, :], bb)
            acc = acc + hx * (g - carry[0, s, :])
            carry[0, s, :] = g
            carry[1, s, :] = b
            carry[2, s, :] = bb
            a = x - pltpu.roll(x, roll_y, 0)
            b = pltpu.roll(a, back_y, 0)
            g = x2 + slope(a, b, a * a + eps2, b * b + eps2)
            acc = acc + hy * (g - pltpu.roll(g, roll_y, 0))
            z = pl.ds(offs[i], NY)
            emit(j, i, x * keep_ref[n, z, :] + (jnp.exp2(arg[n, z, :]) - acc))


def flip(neg, count, i):
    return jnp.where(neg, count - 1 - i, i)


def load_natural(ref, index):
    return lambda o: ref[index, o * PER : (o + 1) * PER, :]


def store_tile(ref, index):
    def store(o, z, value):
        ref[index, o, z * NY : (z + 1) * NY, :] = value

    return store


def start_kernel(info, x, *refs):
    tabs, (tiles, mom, tmp) = refs[:4], refs[4:]
    layers, octants = tiles.shape[0], tiles.shape[1]
    neg, first = info[0] != 0, info[1]
    for j in range(layers):
        nat = flip(neg, layers, j)
        convert(load_natural(x, nat), store_tile(tiles, j), tmp, octants)
        total = 0.0
        for o in range(octants):
            total = total + moments_of(tiles[j, o], tabs[2][first + o])
        mom[nat] = total


def share_kernel(info, ma, mb, scale, heavy, light):
    layers = ma.shape[0]
    neg = info[0] != 0
    row = lax.broadcasted_iota(jnp.int32, (8, LANES), 0)

    def packed(j):
        nat = flip(neg, layers, j)
        return jnp.where(row == 5, scale[nat], ma[nat] + mb[nat])

    for i in range(4):
        heavy[i] = packed(layers - 4 + i)
    for i in range(2):
        light[i] = packed(i)


def first_kernel(info, tiles, h1, l1, ma, mb, scale, *refs):
    tabs = refs[:4]
    new, side, mom, tmp, arg, keep, carry, coef = refs[4:]
    layers, octants = tiles.shape[0], tiles.shape[1]
    neg, first = info[0] != 0, info[1]
    for i in range(2):
        convert(load_natural(h1, flip(neg, 2, i)), store_tile(side, i), tmp, octants)
    convert(load_natural(l1, 0), store_tile(side, 2), tmp, octants)
    js = list(range(layers))
    for j in js:
        nat = flip(neg, layers, j)
        coef[j] = coefficients(ma[nat] + mb[nat], scale[nat])
        mom[nat] = jnp.zeros((8, LANES), F32)
    prepare(js, coef, tabs, keep)

    def get(j):
        return (side, j + 2) if j < 0 else (side, 2) if j == layers else (tiles, j)

    @pl.loop(0, octants)
    def _(o):
        place = place_octant(first + o)

        def emit(j, i, value):
            new[j, o, pl.ds(place[1][i], NY), :] = value

        advance(js, get, o, first + o, place, coef, tabs, arg, keep, carry, emit)
        for j in js:
            nat = flip(neg, layers, j)
            mom[nat] += moments_of(new[j, o], tabs[2][first + o])


def second_kernel(info, tiles, side, h2, l2, sh, sl, new, ma, mb, scale, *refs):
    tabs = refs[:4]
    edge, far, newer, mom, tmp, arg, keep, carry, coef, last = refs[4:]
    layers, octants = tiles.shape[0], tiles.shape[1]
    neg, first = info[0] != 0, info[1]
    for i in range(2):
        convert(load_natural(h2, flip(neg, 2, i)), store_tile(far, i), tmp, octants)
        convert(load_natural(l2, flip(neg, 2, i)), store_tile(last, i), tmp, octants)
    up, down, own = [-2, -1], [layers, layers + 1], list(range(layers))
    outer = {}
    for i in range(2):
        coef[i] = coefficients(sh[2 + i], sh[2 + i, 5:6])
        coef[2 + i] = coefficients(sl[i], sl[i, 5:6])
    for j in own:
        nat = flip(neg, layers, j)
        coef[4 + j] = coefficients(ma[nat] + mb[nat], scale[nat])
    outer = {-2: 0, -1: 1, layers: 2, layers + 1: 3}
    at_outer = {j: coef.at[n] for j, n in outer.items()}
    at_own = {j: coef.at[4 + j] for j in own}
    co = {j: r[...] for j, r in at_outer.items()}
    cn = {j: r[...] for j, r in at_own.items()}
    prepare(up + down, co, tabs, keep)
    prepare(own, cn, tabs, keep.at[4:])
    for n in range(mom.shape[0]):
        mom[n] = jnp.zeros((8, LANES), F32)

    def get0(j):
        if j < -2:
            return far, j + 4
        if j < 0:
            return side, j + 2
        if j > layers:
            return last, j - layers - 1
        return (side, 2) if j == layers else (tiles, j)

    def get1(j):
        return (edge, outer[j]) if j in outer else (new, j)

    @pl.loop(0, octants)
    def _(o):
        octant = first + o
        place = place_octant(octant)

        def emit1(j, i, value):
            edge[outer[j], o, pl.ds(place[1][i], NY), :] = value

        def emit2(j, i, value):
            newer[j, o, pl.ds(place[1][i], NY), :] = value

        advance(up, get0, o, octant, place, co, tabs, arg, keep, carry, emit1)
        advance(down, get0, o, octant, place, co, tabs, arg.at[2:], keep.at[2:], carry, emit1)
        advance(own, get1, o, octant, place, cn, tabs, arg.at[4:], keep.at[4:], carry, emit2)
        for j, n in outer.items():
            mom[2 + flip(neg, layers, j)] += moments_of(edge[n, o], tabs[2][octant])
        for j in own:
            nat = flip(neg, layers, j)
            mom[layers + 4 + nat] += moments_of(newer[j, o], tabs[2][octant])


def third_kernel(info, side, far, h3, sh, *refs):
    tabs = refs[:4]
    rim, tmp, arg, keep, carry, coef, last = refs[4:]
    octants = side.shape[1]
    neg, first = info[0] != 0, info[1]
    for i in range(2):
        convert(load_natural(h3, flip(neg, 2, i)), store_tile(last, i), tmp, octants)
    js = [-4, -3]
    co = {}
    for i, j in enumerate(js):
        co[j] = coefficients(sh[i], sh[i, 5:6])
    prepare(js, co, tabs, keep)

    def get(j):
        return (last, j + 6) if j < -4 else (far, j + 4) if j < -2 else (side, j + 2)

    @pl.loop(0, octants)
    def _(o):
        place = place_octant(first + o)

        def emit(j, i, value):
            rim[j + 4, o, pl.ds(place[1][i], NY), :] = value

        advance(js, get, o, first + o, place, co, tabs, arg, keep, carry, emit)


def last_kernel(info, rim, edge, new, newer, ma, mb, sh, sl, scale, *refs):
    tabs = refs[:4]
    out, tmp, arg, keep, carry, beside, result = refs[4:]
    layers, octants = new.shape[0], new.shape[1]
    neg, first = info[0] != 0, info[1]
    up, down, own = [-2, -1], [layers], list(range(layers))
    outer = {-2: 0, -1: 1, layers: 2, layers + 1: 3}
    co, cn = {}, {}
    for j in up + down:
        slot = 2 + flip(neg, layers, j)
        pace = sl[0, 5:6] if j == layers else sh[4 + j, 5:6]
        co[j] = coefficients(ma[slot] + mb[slot], pace)
    for j in own:
        nat = flip(neg, layers, j)
        cn[j] = coefficients(ma[layers + 4 + nat] + mb[layers + 4 + nat], scale[nat])
    prepare(up + down, co, tabs, keep)
    prepare(own, cn, tabs, keep.at[3:])

    def get1(j):
        return (rim, j + 4) if j < -2 else (edge, outer[j]) if j in outer else (new, j)

    def get2(j):
        return (beside, outer[j]) if j in outer else (newer, j)

    @pl.loop(0, octants)
    def _(o):
        octant = first + o
        place = place_octant(octant)
        starts = [place[1][i] // NY for i in range(NZ)]

        def emit2(j, i, value):
            beside[outer[j], o, pl.ds(place[1][i], NY), :] = value

        def emit3(j, i, value):
            result[j, o, pl.ds(starts[i], NY, stride=NZ), :] = value

        advance(up, get1, o, octant, place, co, tabs, arg, keep, carry, emit2)
        advance(down, get1, o, octant, place, co, tabs, arg.at[2:], keep.at[2:], carry, emit2)
        advance(own, get2, o, octant, place, cn, tabs, arg.at[3:], keep.at[3:], carry, emit3)

    for j in own:
        nat = flip(neg, layers, j)
        for o in range(octants):
            out[nat, o * PER : (o + 1) * PER, :] = result[j, o].T[:PER]


def scratch(octants, layers, extra=()):
    square = (LANES, LANES)
    return [
        pltpu.VMEM((octants, *square), F32),
        pltpu.VMEM((layers, *square), F32),
        pltpu.VMEM((layers, *square), F32),
        pltpu.VMEM((3, *square), F32),
        *extra,
    ]


def run(body, name, args, outs, scratch_shapes):
    return pl.pallas_call(
        body,
        name=name,
        out_shape=[jax.ShapeDtypeStruct(shape, F32) for shape in outs],
        in_specs=[SMEM] + [VMEM] * (len(args) - 1),
        out_specs=[VMEM] * len(outs),
        scratch_shapes=scratch_shapes,
        compiler_params=pltpu.CompilerParams(vmem_limit_bytes=24 * 2**20),
    )(*args)


def exchange(part, axis):
    count = lax.axis_size(axis)
    if count == 1:
        return part, jnp.zeros_like(part)
    if count & (count - 1):
        return lax.psum(part, axis), jnp.zeros_like(part)
    bit = 1
    while True:
        other = lax.ppermute(part, axis, [(i, i ^ bit) for i in range(count)])
        bit *= 2
        if bit == count:
            return part, other
        part = part + other


def per_device(distribution, collision_scale):
    vel_count, layers, _ = distribution.shape
    oct_count, ring = lax.axis_size("oct"), lax.axis_size("space")
    octants = vel_count // PER
    assert vel_count % PER == 0 and oct_count % 2 == 0 and layers >= 6
    first = lax.axis_index("oct") * octants
    neg = first // 4 % 2
    info = jnp.stack([neg, first]).astype(jnp.int32)
    toward = []
    for o in range(oct_count):
        step = -1 if o * octants // 4 % 2 else 1
        for s in range(ring):
            toward.append((o * ring + s, o * ring + (s + step) % ring))
    against = [(target, source) for source, target in toward]

    def send(block, pairs):
        return lax.ppermute(block, ("oct", "space"), pairs)

    def cut(low, high, count):
        start = jnp.where(neg == 1, low, high)
        return lax.dynamic_slice_in_dim(x, start, count, 0)

    x = jnp.transpose(distribution, (1, 0, 2))
    h1 = send(cut(0, layers - 2, 2), toward)
    l1 = send(cut(layers - 1, 0, 1), against)
    h2 = send(cut(2, layers - 4, 2), toward)
    l2 = send(cut(layers - 3, 1, 2), against)
    scale = collision_scale.reshape(layers, NY, NZ).transpose(0, 2, 1).reshape(layers, 1, LANES)
    tabs = tables()
    tile = (octants, LANES, LANES)
    coef = pltpu.VMEM((layers + 4, 32, LANES), BF16)
    tiles, m0 = run(
        start_kernel,
        "start",
        (info, x, *tabs),
        [(layers, *tile), (layers, 8, LANES)],
        [pltpu.VMEM(tile, F32)],
    )
    m0 = exchange(m0, "oct")
    sh, sl = run(
        share_kernel, "share", (info, *m0, scale), [(4, 8, LANES), (2, 8, LANES)], []
    )
    sh, sl = send(sh, toward), send(sl, against)
    h3 = send(cut(4, layers - 6, 2), toward)
    new, side, m1 = run(
        first_kernel,
        "first",
        (info, tiles, h1, l1, *m0, scale, *tabs),
        [(layers, *tile), (3, *tile), (layers, 8, LANES)],
        scratch(octants, layers, [coef]),
    )
    m1 = exchange(m1, "oct")
    edge, far, newer, m2 = run(
        second_kernel,
        "second",
        (info, tiles, side, h2, l2, sh, sl, new, *m1, scale, *tabs),
        [(4, *tile), (2, *tile), (layers, *tile), (2 * layers + 4, 8, LANES)],
        scratch(octants, layers + 4, [coef, pltpu.VMEM((2, *tile), F32)]),
    )
    m2 = exchange(m2, "oct")
    (rim,) = run(
        third_kernel,
        "third",
        (info, side, far, h3, sh, *tabs),
        [(2, *tile)],
        scratch(octants, 2, [coef, pltpu.VMEM((2, *tile), F32)]),
    )
    (out,) = run(
        last_kernel,
        "last",
        (info, rim, edge, new, newer, *m2, sh, sl, scale, *tabs),
        [(layers, vel_count, LANES)],
        scratch(
            octants, layers + 3, [pltpu.VMEM((3, *tile), F32), pltpu.VMEM((layers, *tile), F32)]
        ),
    )
    return jnp.transpose(out, (1, 0, 2))


def solution(mesh):
    return jax.shard_map(
        per_device,
        mesh=mesh,
        in_specs=(P("oct", "space", None), P(None, "space", None)),
        out_specs=P("oct", "space", None),
        check_vma=False,
    )
```

profile of v0, /device:TPU:0, one launch (start us, length us, event | category | flops | bytes accessed | tf_op | source)
XLA Modules:
  0.0 66.6 jit_solution(10245417217880752167)
XLA Ops:
  0.0 3.1 %dynamic-slice_bitcast_fusion = (f32[2,500,128]{2,1,0:T(8,128)}, f32[2,500,128]{2,1,0:T(8,128)}, f32[2,500,128]{2,1,0:T(8,128)}, f32[2,500,128]{2,1,0:T(8,128)}) fusion(f32[500,6,128]{2,0,1:T(8,128)} %param.6, s32[]{:T(128)S(6)} %select_n.35, s32[]{:T(128)S(6)} %select_n.32, s32[]{:T(128)S(6)} %select_n.34), kind=kLoop, calls=%fused_computation | loop fusion | bytes 4096012 | tf_op jit(solution)/shard_map/dynamic_slice | solution.py:442
  3.1 0.5 collective-permute-start
  3.6 2.6 %collective-permute-start.8 = (f32[2,500,128]{2,1,0:T(8,128)}, f32[2,500,128]{2,1,0:T(8,128)}, u32[]{:S(2)}, u32[]{:S(2)}) collective-permute-start(f32[2,500,128]{2,1,0:T(8,128)} %get-tuple-element.27), channel_id=1, source_target_pairs={{0,1},{1,2},{2,3},{3,4},{4,5},{5,6},{6,7},{7,8},{8,9},{9,10},{10,1... | collective-permute-start | bytes 1536008 | tf_op jit(solution)/shard_map/ppermute | solution.py:438
  6.3 4.4 %collective-permute-start.4 = (f32[2,500,128]{2,1,0:T(8,128)}, f32[2,500,128]{2,1,0:T(8,128)}, u32[]{:S(2)}, u32[]{:S(2)}) collective-permute-start(f32[2,500,128]{2,1,0:T(8,128)} %get-tuple-element.30), channel_id=1, source_target_pairs={{1,0},{2,1},{3,2},{4,3},{5,4},{6,5},{7,6},{8,7},{9,8},{10,9},{11,1... | collective-permute-start | bytes 1536008 | tf_op jit(solution)/shard_map/ppermute | solution.py:438
  10.7 0.1 pad_add_fusion.info
  10.8 1.8 %start.1 = (f32[6,4,128,128]{3,2,1,0:T(8,128)S(1)}, f32[6,8,128]{2,1,0:T(8,128)S(1)}) custom-call(s32[2]{0:T(128)S(1)} %pad_add_fusion.info, f32[6,500,128]{2,1,0:T(8,128)S(1)} %bitcast.15, bf16[8,32,128]{2,1,0:T(8,128)(2,1)S(1)} %copy-done.1, bf16[32,128]{1,0:T(8,128)(2,1)S(1)} %copy-done.4, bf16[8,16,128]{2,1,0:T(8,128)(2,1)S(1)} %copy-done.3, ...), custom_call_target="tpu_custom_call" | custom-call | tf_op jit(solution)/shard_map/start/pallas_call | solution.py:396
  12.6 0.6 collective-permute-start.2
  13.1 0.7 %dynamic-slice_bitcast_fusion.3 = f32[1,500,128]{2,1,0:T(8,128)} fusion(f32[500,6,128]{2,0,1:T(8,128)S(1)} %copy-done, s32[]{:T(128)S(6)} %select_n.33), kind=kLoop, calls=%fused_computation.4 | loop fusion | bytes 512004 | tf_op jit(solution)/shard_map/dynamic_slice | solution.py:442
  13.8 2.6 %collective-permute-done.2.mb = f32[6,8,128]{2,1,0:T(8,128)S(1)} collective-permute-done((f32[6,8,128]{2,1,0:T(8,128)S(1)}, f32[6,8,128]{2,1,0:T(8,128)S(1)}, u32[]{:S(2)}, u32[]{:S(2)}) %collective-permute-start.2) | collective-permute-done | bytes 24608 | tf_op jit(solution)/shard_map/ppermute | solution.py:415
  16.4 2.0 %collective-permute-start.1 = (f32[1,500,128]{2,1,0:T(8,128)}, f32[1,500,128]{2,1,0:T(8,128)S(1)}, u32[]{:S(2)}, u32[]{:S(2)}) collective-permute-start(f32[1,500,128]{2,1,0:T(8,128)} %dynamic-slice_bitcast_fusion.3), channel_id=1, source_target_pairs={{1,0},{2,1},{3,2},{4,3},{5,4},{6,5},{7,6},{8,7},{9,8},{10,9},{11,1... | collective-permute-start | bytes 768008 | tf_op jit(solution)/shard_map/ppermute | solution.py:438
  18.4 0.1 reshape.7
  18.5 0.1 copy.8
  18.6 0.1 reshape.9.scale
  18.7 0.6 share.1
  19.3 3.3 %collective-permute-done.1.l1 = f32[1,500,128]{2,1,0:T(8,128)S(1)} collective-permute-done((f32[1,500,128]{2,1,0:T(8,128)}, f32[1,500,128]{2,1,0:T(8,128)S(1)}, u32[]{:S(2)}, u32[]{:S(2)}) %collective-permute-start.1) | collective-permute-done | bytes 256032 | tf_op jit(solution)/shard_map/ppermute | solution.py:438
  22.6 4.6 %collective-permute-start.6 = (f32[2,8,128]{2,1,0:T(8,128)S(1)}, f32[2,8,128]{2,1,0:T(8,128)S(1)}, u32[]{:S(2)}, u32[]{:S(2)}) collective-permute-start(f32[2,8,128]{2,1,0:T(8,128)S(1)} %get-tuple-element.20), channel_id=1, source_target_pairs={{1,0},{2,1},{3,2},{4,3},{5,4},{6,5},{7,6},{8,7},{9,8},{10,9},{11,1... | collective-permute-start | bytes 24584 | tf_op jit(solution)/shard_map/ppermute | solution.py:438
  27.2 6.2 %first.1 = (f32[6,4,128,128]{3,2,1,0:T(8,128)S(1)}, f32[3,4,128,128]{3,2,1,0:T(8,128)S(1)}, f32[6,8,128]{2,1,0:T(8,128)S(1)}) custom-call(s32[2]{0:T(128)S(1)} %pad_add_fusion.info, f32[6,4,128,128]{3,2,1,0:T(8,128)S(1)} %get-tuple-element.16.tiles, f32[2,500,128]{2,1,0:T(8,128)} %collective-permute-done.h1, f32[1,500,128]{2,1,0:T(8,128)S(1)} %collective-permute-done.1.l1, ...), custom_call_target="tpu_custom_call" | custom-call | tf_op jit(solution)/shard_map/first/pallas_call | solution.py:396
  33.4 7.1 %collective-permute-start.7 = (f32[6,8,128]{2,1,0:T(8,128)S(1)}, f32[6,8,128]{2,1,0:T(8,128)S(1)}, u32[]{:S(2)}, u32[]{:S(2)}) collective-permute-start(f32[6,8,128]{2,1,0:T(8,128)S(1)} %get-tuple-element.22.ma), channel_id=1, source_target_pairs={{0,16},{16,0},{1,17},{17,1},{2,18},{18,2},{3,19},{19,3},{4,20},{20... | collective-permute-start | bytes 73736 | tf_op jit(solution)/shard_map/ppermute | solution.py:415
  40.5 2.1 %collective-permute-start.5 = (f32[4,8,128]{2,1,0:T(8,128)S(1)}, f32[4,8,128]{2,1,0:T(8,128)S(1)}, u32[]{:S(2)}, u32[]{:S(2)}) collective-permute-start(f32[4,8,128]{2,1,0:T(8,128)S(1)} %get-tuple-element.19), channel_id=1, source_target_pairs={{0,1},{1,2},{2,3},{3,4},{4,5},{5,6},{6,7},{7,8},{8,9},{9,10},{10,1... | collective-permute-start | bytes 49160 | tf_op jit(solution)/shard_map/ppermute | solution.py:438
  42.6 3.8 %collective-permute-done.5.sh = f32[4,8,128]{2,1,0:T(8,128)S(1)} collective-permute-done((f32[4,8,128]{2,1,0:T(8,128)S(1)}, f32[4,8,128]{2,1,0:T(8,128)S(1)}, u32[]{:S(2)}, u32[]{:S(2)}) %collective-permute-start.5) | collective-permute-done | bytes 16416 | tf_op jit(solution)/shard_map/ppermute | solution.py:438
  46.4 8.6 %second.1 = (f32[4,4,128,128]{3,2,1,0:T(8,128)S(1)}, f32[2,4,128,128]{3,2,1,0:T(8,128)S(1)}, f32[6,4,128,128]{3,2,1,0:T(8,128)S(1)}, f32[16,8,128]{2,1,0:T(8,128)S(1)}) custom-call(s32[2]{0:T(128)S(1)} %pad_add_fusion.info, f32[6,4,128,128]{3,2,1,0:T(8,128)S(1)} %get-tuple-element.16.tiles, f32[3,4,128,128]{3,2,1,0:T(8,128)S(1)} %get-tuple-element.18.side, ...), custom_call_target="tpu_custom_call" | custom-call | tf_op jit(solution)/shard_map/second/pallas_call | solution.py:396
  55.1 2.7 %third.1.rim = f32[2,4,128,128]{3,2,1,0:T(8,128)S(1)} custom-call(s32[2]{0:T(128)S(1)} %pad_add_fusion.info, f32[3,4,128,128]{3,2,1,0:T(8,128)S(1)} %get-tuple-element.18.side, f32[2,4,128,128]{3,2,1,0:T(8,128)S(1)} %get-tuple-element.23.far, f32[2,500,128]{2,1,0:T(8,128)} %collective-permute-done.8.h3, f32[4,8,128]{2,1,0:T(8,128)S(1)} %collective-permute-done.5.sh, ...), custom_call_target="tpu_custom_call" | custom-call | tf_op jit(solution)/shard_map/third/pallas_call | solution.py:396
  57.8 1.5 %collective-permute-done.9.mb = f32[16,8,128]{2,1,0:T(8,128)S(1)} collective-permute-done((f32[16,8,128]{2,1,0:T(8,128)S(1)}, f32[16,8,128]{2,1,0:T(8,128)S(1)}, u32[]{:S(2)}, u32[]{:S(2)}) %collective-permute-start.9) | collective-permute-done | bytes 65568 | tf_op jit(solution)/shard_map/ppermute | solution.py:415
  59.3 7.3 %last.1 = f32[6,500,128]{2,1,0:T(8,128)} custom-call(s32[2]{0:T(128)S(1)} %pad_add_fusion.info, f32[2,4,128,128]{3,2,1,0:T(8,128)S(1)} %third.1.rim, f32[4,4,128,128]{3,2,1,0:T(8,128)S(1)} %get-tuple-element.24.edge, f32[6,4,128,128]{3,2,1,0:T(8,128)S(1)} %get-tuple-element.21.new, f32[6,4,128,128]{3,2,1,0:T(8,128)S(1)} %get-tuple-element.25.newer, ...), custom_call_target="tpu_custom_call" | custom-call | tf_op jit(solution)/shard_map/last/pallas_call | solution.py:396
  (21 shorter events, 0.2 us)
Async XLA Ops:
  0.0 10.7 %copy-start = (f32[500,6,128]{2,0,1:T(8,128)S(1)}, f32[500,6,128]{2,0,1:T(8,128)}, u32[]{:S(2)}) copy-start(f32[500,6,128]{2,0,1:T(8,128)} %param.6) | copy-start | bytes 4608004
  0.0 10.7 %copy-start.1 = (bf16[8,32,128]{2,1,0:T(8,128)(2,1)S(1)}, bf16[8,32,128]{2,1,0:T(8,128)(2,1)}, u32[]{:S(2)}) copy-start(bf16[8,32,128]{2,1,0:T(8,128)(2,1)} %constant.52.clone.refs_0_) | copy-start | bytes 196612
  0.0 10.7 %copy-start.2 = (f32[8,8,128]{2,1,0:T(8,128)S(1)}, f32[8,8,128]{2,1,0:T(8,128)}, u32[]{:S(2)}) copy-start(f32[8,8,128]{2,1,0:T(8,128)} %constant.55.clone.refs_3_) | copy-start | bytes 98308
  0.0 10.7 %copy-start.3 = (bf16[8,16,128]{2,1,0:T(8,128)(2,1)S(1)}, bf16[8,16,128]{2,1,0:T(8,128)(2,1)}, u32[]{:S(2)}) copy-start(bf16[8,16,128]{2,1,0:T(8,128)(2,1)} %constant.54.clone.refs_2_) | copy-start | bytes 98308
  0.0 10.7 %copy-start.4 = (bf16[32,128]{1,0:T(8,128)(2,1)S(1)}, bf16[32,128]{1,0:T(8,128)(2,1)}, u32[]{:S(2)}) copy-start(bf16[32,128]{1,0:T(8,128)(2,1)} %constant.53.clone.refs_1_) | copy-start | bytes 24580
  3.1 15.3 %copy-start.5 = (f32[1,6,128]{2,0,1:T(1,128)S(1)}, f32[1,6,128]{2,0,1:T(1,128)}, u32[]{:S(2)}) copy-start(f32[1,6,128]{2,0,1:T(1,128)} %param.7) | copy-start | bytes 9220
  3.1 24.1 %collective-permute-start = (f32[2,500,128]{2,1,0:T(8,128)}, f32[2,500,128]{2,1,0:T(8,128)}, u32[]{:S(2)}, u32[]{:S(2)}) collective-permute-start(f32[2,500,128]{2,1,0:T(8,128)} %get-tuple-element.29), channel_id=1, source_target_pairs={{0,1},{1,2},{2,3},{3,4},{4,5},{5,6},{6,7},{7,8},{8,9},{9,10},{10,1... | collective-permute-start | bytes 1536008 | tf_op jit(solution)/shard_map/ppermute | solution.py:438
  3.6 51.5 %collective-permute-start.8 = (f32[2,500,128]{2,1,0:T(8,128)}, f32[2,500,128]{2,1,0:T(8,128)}, u32[]{:S(2)}, u32[]{:S(2)}) collective-permute-start(f32[2,500,128]{2,1,0:T(8,128)} %get-tuple-element.27), channel_id=1, source_target_pairs={{0,1},{1,2},{2,3},{3,4},{4,5},{5,6},{6,7},{7,8},{8,9},{9,10},{10,1... | collective-permute-start | bytes 1536008 | tf_op jit(solution)/shard_map/ppermute | solution.py:438
  6.2 40.2 %collective-permute-start.3 = (f32[2,500,128]{2,1,0:T(8,128)}, f32[2,500,128]{2,1,0:T(8,128)}, u32[]{:S(2)}, u32[]{:S(2)}) collective-permute-start(f32[2,500,128]{2,1,0:T(8,128)} %get-tuple-element.28), channel_id=1, source_target_pairs={{0,1},{1,2},{2,3},{3,4},{4,5},{5,6},{6,7},{7,8},{8,9},{9,10},{10,1... | collective-permute-start | bytes 1536008 | tf_op jit(solution)/shard_map/ppermute | solution.py:438
  6.3 40.1 %collective-permute-start.4 = (f32[2,500,128]{2,1,0:T(8,128)}, f32[2,500,128]{2,1,0:T(8,128)}, u32[]{:S(2)}, u32[]{:S(2)}) collective-permute-start(f32[2,500,128]{2,1,0:T(8,128)} %get-tuple-element.30), channel_id=1, source_target_pairs={{1,0},{2,1},{3,2},{4,3},{5,4},{6,5},{7,6},{8,7},{9,8},{10,9},{11,1... | collective-permute-start | bytes 1536008 | tf_op jit(solution)/shard_map/ppermute | solution.py:438
  12.6 3.9 %collective-permute-start.2 = (f32[6,8,128]{2,1,0:T(8,128)S(1)}, f32[6,8,128]{2,1,0:T(8,128)S(1)}, u32[]{:S(2)}, u32[]{:S(2)}) collective-permute-start(f32[6,8,128]{2,1,0:T(8,128)S(1)} %get-tuple-element.17.ma), channel_id=1, source_target_pairs={{0,16},{16,0},{1,17},{17,1},{2,18},{18,2},{3,19},{19,3},{4,20},{20... | collective-permute-start | bytes 73736 | tf_op jit(solution)/shard_map/ppermute | solution.py:415
  16.4 6.2 %collective-permute-start.1 = (f32[1,500,128]{2,1,0:T(8,128)}, f32[1,500,128]{2,1,0:T(8,128)S(1)}, u32[]{:S(2)}, u32[]{:S(2)}) collective-permute-start(f32[1,500,128]{2,1,0:T(8,128)} %dynamic-slice_bitcast_fusion.3), channel_id=1, source_target_pairs={{1,0},{2,1},{3,2},{4,3},{5,4},{6,5},{7,6},{8,7},{9,8},{10,9},{11,1... | collective-permute-start | bytes 768008 | tf_op jit(solution)/shard_map/ppermute | solution.py:438
  22.6 17.9 %collective-permute-start.6 = (f32[2,8,128]{2,1,0:T(8,128)S(1)}, f32[2,8,128]{2,1,0:T(8,128)S(1)}, u32[]{:S(2)}, u32[]{:S(2)}) collective-permute-start(f32[2,8,128]{2,1,0:T(8,128)S(1)} %get-tuple-element.20), channel_id=1, source_target_pairs={{1,0},{2,1},{3,2},{4,3},{5,4},{6,5},{7,6},{8,7},{9,8},{10,9},{11,1... | collective-permute-start | bytes 24584 | tf_op jit(solution)/shard_map/ppermute | solution.py:438
  33.4 13.0 %collective-permute-start.7 = (f32[6,8,128]{2,1,0:T(8,128)S(1)}, f32[6,8,128]{2,1,0:T(8,128)S(1)}, u32[]{:S(2)}, u32[]{:S(2)}) collective-permute-start(f32[6,8,128]{2,1,0:T(8,128)S(1)} %get-tuple-element.22.ma), channel_id=1, source_target_pairs={{0,16},{16,0},{1,17},{17,1},{2,18},{18,2},{3,19},{19,3},{4,20},{20... | collective-permute-start | bytes 73736 | tf_op jit(solution)/shard_map/ppermute | solution.py:415
  40.5 5.9 %collective-permute-start.5 = (f32[4,8,128]{2,1,0:T(8,128)S(1)}, f32[4,8,128]{2,1,0:T(8,128)S(1)}, u32[]{:S(2)}, u32[]{:S(2)}) collective-permute-start(f32[4,8,128]{2,1,0:T(8,128)S(1)} %get-tuple-element.19), channel_id=1, source_target_pairs={{0,1},{1,2},{2,3},{3,4},{4,5},{5,6},{6,7},{7,8},{8,9},{9,10},{10,1... | collective-permute-start | bytes 49160 | tf_op jit(solution)/shard_map/ppermute | solution.py:438
  55.0 4.3 %collective-permute-start.9 = (f32[16,8,128]{2,1,0:T(8,128)S(1)}, f32[16,8,128]{2,1,0:T(8,128)S(1)}, u32[]{:S(2)}, u32[]{:S(2)}) collective-permute-start(f32[16,8,128]{2,1,0:T(8,128)S(1)} %get-tuple-element.26.ma), channel_id=1, source_target_pairs={{0,16},{16,0},{1,17},{17,1},{2,18},{18,2},{3,19},{19,3},{4,20},{20... | collective-permute-start | bytes 196616 | tf_op jit(solution)/shard_map/ppermute | solution.py:415
where the time goes:
time: 66.8 us; the launch traced here: 66.6 us
  Pallas kernels  27.1 us (41%)
  starting transfers between devices  24 us (36%)
  waiting for transfers between devices  11.2 us (17%)
  local copies, waits for them, and re-layouts  4.06 us (6%)
    pallas_call x6, Pallas kernels, run(): pl.pallas_call(body, name=name, out_shape=[jax.ShapeDtypeStruct(shape, F3...  27.1 us
    ppermute x7, starting transfers between devices, send(): return lax.ppermute(block, ('oct', 'space'), pairs)  16.3 us
    ppermute x3, starting transfers between devices, exchange(): other = lax.ppermute(part, axis, [(i, i ^ bit) for i in range(count)])  7.74 us
    ppermute x7, waiting for transfers between devices, send(): return lax.ppermute(block, ('oct', 'space'), pairs)  7.1 us
    ppermute x3, waiting for transfers between devices, exchange(): other = lax.ppermute(part, axis, [(i, i ^ bit) for i in range(count)])  4.12 us
    dynamic_slice x2, local copies, waits for them, and re-layouts, cut(): return lax.dynamic_slice_in_dim(x, start, count, 0)  3.79 us
  transfers between devices with their start and end apart: 10, of which 4 were waited for; matrix products, arithmetic and copies ran while one was open for 2% of the time, Pallas kernels for 30%

commit v1 on v0

v1 whole, which is shorter than its diff:
```python
import math

import jax
import jax.numpy as jnp
import numpy as np
from jax import lax
from jax.experimental import pallas as pl
from jax.experimental.pallas import tpu as pltpu
from jax.sharding import PartitionSpec as P


NV = 10
NZ = 16
NY = 8
HALF = NV // 2
PER = HALF**3
LANES = 128

vel_bound = 4.0
courant = 0.08
time_step = 0.08
base_rate = 0.25
visc_index = 0.81
limiter_eps = 0.01
spacing = 2.0 * vel_bound / NV
quad = spacing**3 * (2.0 * math.pi) ** (-1.5)
unit = 0.5 * spacing
log2e = math.log2(math.e)

VMEM = pl.BlockSpec(memory_space=pltpu.VMEM)
HBM = pl.BlockSpec(memory_space=pltpu.HBM)
SMEM = pl.BlockSpec(memory_space=pltpu.SMEM)
NT = (((1,), (1,)), ((), ()))
TN = (((0,), (0,)), ((), ()))
F32 = jnp.float32
BF16 = jnp.bfloat16


def table():
    within = np.arange(PER)
    size = np.stack([within // HALF**2, within // HALF % HALF, within % HALF]) * 2 + 1
    feature = np.zeros((9, 8, LANES), np.float32)
    for octant in range(8):
        sign = np.array([1 - 2 * (octant >> 2 & 1), 1 - 2 * (octant >> 1 & 1), 1 - 2 * (octant & 1)])
        feature[octant, 0, :PER] = 1
        feature[octant, 1:4, :PER] = size * sign[:, None]
        feature[octant, 4, :PER] = (size * size).sum(0)
    feature[8, 5] = 1
    pad = np.zeros_like(feature)
    return jnp.asarray(np.concatenate([feature, feature, feature, pad, feature, pad], axis=1), BF16)


def phi(tab, octant):
    return tab[octant, 0:32]


def weight(tab, octant):
    return tab[octant, 32:48]


def slope(left, right, left_sq, right_sq):
    return (left * right) * (left + right) * (1.0 / (left_sq + right_sq))


def place_octant(octant):
    pos_y = octant // 2 % 2 == 0
    pos_z = octant % 2 == 0
    roll_y = jnp.where(pos_y, 1, NY - 1)
    first = jnp.where(pos_z, 0, (NZ - 1) * NY)
    pace = jnp.where(pos_z, NY, -NY)
    offs = [pl.multiple_of(first + i * pace, NY) for i in range(NZ)]
    return roll_y, offs


def convert(load, store, tmp, octants):
    for o in range(octants):
        x = load(o)
        x = jnp.concatenate([x, jnp.zeros((LANES - PER, LANES), F32)], 0)
        tmp[o] = x.T
        for z in range(NZ):
            store(o, z, tmp[o, pl.ds(z, NY, stride=NZ), :])


def coefficients(total, scale):
    m0 = total[0:1]
    inv = 1.0 / m0
    ux = unit * total[1:2] * inv
    uy = unit * total[2:3] * inv
    uz = unit * total[3:4] * inv
    square = ux * ux + uy * uy + uz * uz
    temper = (unit * unit * total[4:5] * inv - square) * (1.0 / 3.0)
    log_t = jnp.log2(temper)
    density = quad * m0
    pace = (time_step * base_rate) * scale * density
    keep = 1.0 - pace * jnp.exp2((1.0 - visc_index) * log_t)
    beta = log2e / temper
    c0 = jnp.log2(pace * density) + (1.0 - visc_index - 1.5) * log_t - 0.5 * beta * square
    slow = unit * beta
    row = lax.broadcasted_iota(jnp.int32, (8, LANES), 0)
    c = jnp.where(row == 0, c0, 0.0)
    c = jnp.where(row == 1, slow * ux, c)
    c = jnp.where(row == 2, slow * uy, c)
    c = jnp.where(row == 3, slow * uz, c)
    c = jnp.where(row == 4, (-0.5 * unit) * slow, c)
    c = jnp.where(row == 5, keep, c)
    high = c.astype(BF16).astype(F32)
    rest = c - high
    middle = rest.astype(BF16).astype(F32)
    low = rest - middle
    return jnp.concatenate([high, middle, low, jnp.zeros_like(c)], 0).astype(BF16)


def moments_of(x, rows):
    high = x.astype(BF16)
    low = (x - high.astype(F32)).astype(BF16)
    m = lax.dot_general(rows, high, NT, preferred_element_type=F32)
    m = m + lax.dot_general(rows, low, NT, preferred_element_type=F32)
    return m[:8]


def prepare(js, coef, tab, keep_ref):
    for n, j in enumerate(js):
        keep_ref[n] = lax.dot_general(coef[j], phi(tab, 8), TN, preferred_element_type=F32)


def advance(js, get, o, octant, place, coef, tab, arg, keep_ref, carry, emit):
    roll_y, offs = place
    back_y = NY - roll_y
    half = (0.5 * courant * unit) * jnp.abs(weight(tab, octant).astype(F32))
    hx, hy, hz = half[1:2], half[2:3], half[3:4]
    for n, j in enumerate(js):
        arg[n] = lax.dot_general(coef[j], phi(tab, octant), TN, preferred_element_type=F32)

    def rd(j, i):
        ref, index = get(j)
        return ref[index, o, pl.ds(offs[i % NZ], NY), :]

    def square(d, index):
        return d * d + limiter_eps if index % 2 == 0 else d * d

    j = js[0] - 1
    for i in range(NZ):
        x = rd(j, i)
        a = x - rd(j - 1, i)
        b = rd(j + 1, i) - x
        bb = square(b, j)
        s = pl.ds(i * NY, NY)
        carry[0, s, :] = (x + x) + slope(a, b, square(a, j - 1), bb)
        carry[1, s, :] = b
        carry[2, s, :] = bb
    for n, j in enumerate(js):
        xm2, xm1, x0 = rd(j, NZ - 2), rd(j, NZ - 1), rd(j, 0)
        am, az = xm1 - xm2, x0 - xm1
        ez = square(az, NZ - 1)
        gz = (xm1 + xm1) + slope(am, az, square(am, NZ - 2), ez)
        for i in range(NZ):
            s = pl.ds(i * NY, NY)
            x, xn = x0, rd(j, i + 1)
            x2 = x + x
            an = xn - x
            en = square(an, i)
            gn = x2 + slope(az, an, ez, en)
            acc = hz * (gn - gz)
            az, ez, gz, x0 = an, en, gn, xn
            b = rd(j + 1, i) - x
            bb = square(b, j)
            g = x2 + slope(carry[1, s, :], b, carry[2, s, :], bb)
            acc = acc + hx * (g - carry[0, s, :])
            carry[0, s, :] = g
            carry[1, s, :] = b
            carry[2, s, :] = bb
            a = x - pltpu.roll(x, roll_y, 0)
            aa = a * a + 0.5 * limiter_eps
            g = x2 + slope(a, pltpu.roll(a, back_y, 0), aa, pltpu.roll(aa, back_y, 0))
            acc = acc + hy * (g - pltpu.roll(g, roll_y, 0))
            z = pl.ds(offs[i], NY)
            emit(j, i, x * keep_ref[n, z, :] + (jnp.exp2(arg[n, z, :]) - acc))


def flip(neg, count, i):
    return jnp.where(neg, count - 1 - i, i)


def load_natural(ref, index):
    return lambda o: ref[index, o * PER : (o + 1) * PER, :]


def store_tile(ref, index):
    def store(o, z, value):
        ref[index, o, z * NY : (z + 1) * NY, :] = value

    return store


def cut_kernel(info, x, h1, l1, copy, sems, out_sems):
    layers = copy.shape[0]
    neg = info[0] != 0
    base = jnp.where(neg, 0, layers - 2)
    order = [layers - 2, layers - 1, 0, *range(1, layers - 2)]
    places = [flip(neg, layers, j) for j in order]
    loads = [pltpu.make_async_copy(x.at[n], copy.at[n], sems.at[i]) for i, n in enumerate(places)]
    targets = [h1.at[places[0] - base], h1.at[places[1] - base], l1.at[0]]
    stores = [
        pltpu.make_async_copy(copy.at[places[i]], target, out_sems.at[i])
        for i, target in enumerate(targets)
    ]
    for load in loads:
        load.start()
    for load, store in zip(loads, stores):
        load.wait()
        store.start()
    for load in loads[3:]:
        load.wait()
    for store in stores:
        store.wait()


def start_kernel(info, x, raw, tab, tiles, mom, scale, h2, h3, l2, tmp, sems):
    layers, octants = tiles.shape[0], tiles.shape[1]
    neg, first = info[0] != 0, info[1]
    starts = [jnp.where(neg, 2, layers - 4), jnp.where(neg, 4, layers - 6), jnp.where(neg, layers - 3, 1)]
    copies = [
        pltpu.make_async_copy(x.at[pl.ds(begin, 2)], target, sems.at[i])
        for i, (begin, target) in enumerate(zip(starts, (h2, h3, l2)))
    ]
    for c in copies:
        c.start()
    for j in range(layers):
        nat = flip(neg, layers, j)
        convert(load_natural(x, nat), store_tile(tiles, j), tmp, octants)
        total = 0.0
        for o in range(octants):
            total = total + moments_of(tiles[j, o], weight(tab, first + o))
        mom[nat] = total
    padded = jnp.concatenate([raw[0], jnp.zeros((LANES - layers, LANES), F32)], 0)
    tmp[0] = padded.T
    mixed = jnp.concatenate([tmp[0, pl.ds(z, NY, stride=NZ), :] for z in range(NZ)], 0).T
    for n in range(layers):
        scale[n] = mixed[n : n + 1]
    for c in copies:
        c.wait()


def share_kernel(ma, mb, scale, out):
    row = lax.broadcasted_iota(jnp.int32, (8, LANES), 0)
    for n in range(ma.shape[0]):
        out[n] = jnp.where(row == 5, scale[n], ma[n] + mb[n])


def first_kernel(info, tiles, h1, l1, ma, mb, scale, *refs):
    tab = refs[0]
    new, side, mom, tmp, arg, keep, carry = refs[1:]
    layers, octants = tiles.shape[0], tiles.shape[1]
    neg, first = info[0] != 0, info[1]
    for i in range(2):
        convert(load_natural(h1, flip(neg, 2, i)), store_tile(side, i), tmp, octants)
    convert(load_natural(l1, 0), store_tile(side, 2), tmp, octants)
    js = list(range(layers))
    co = {}
    for j in js:
        nat = flip(neg, layers, j)
        co[j] = coefficients(ma[nat] + mb[nat], scale[nat])
        mom[nat] = jnp.zeros((8, LANES), F32)
    prepare(js, co, tab, keep)
    outer = {-2: 0, -1: 1, layers: 2}

    def get(j):
        return (side, outer[j]) if j in outer else (tiles, j)

    @pl.loop(0, octants)
    def _(o):
        octant = first + o
        place = place_octant(octant)

        def emit(j, i, value):
            new[j, o, pl.ds(place[1][i], NY), :] = value

        advance(js, get, o, octant, place, co, tab, arg, keep, carry, emit)
        for j in js:
            mom[flip(neg, layers, j)] += moments_of(new[j, o], weight(tab, octant))


def edge_kernel(info, tiles, side, h2, l2, up_share, down_share, *refs):
    tab = refs[0]
    edge, far, mom, tmp, arg, keep, carry, below = refs[1:]
    layers, octants = tiles.shape[0], tiles.shape[1]
    neg, first = info[0] != 0, info[1]
    for i in range(2):
        convert(load_natural(h2, flip(neg, 2, i)), store_tile(far, i), tmp, octants)
        convert(load_natural(l2, flip(neg, 2, i)), store_tile(below, i), tmp, octants)
    up, down = [-2, -1], [layers, layers + 1]
    outer = {-2: 0, -1: 1, layers: 2, layers + 1: 3}
    co = {}
    for j in outer:
        if j < 0:
            known = up_share[flip(neg, layers, layers + j)]
        else:
            known = down_share[flip(neg, layers, j - layers)]
        co[j] = coefficients(known, known[5:6])
    prepare(up + down, co, tab, keep)
    for n in range(4):
        mom[n] = jnp.zeros((8, LANES), F32)

    def get(j):
        if j < -2:
            return far, j + 4
        if j < 0:
            return side, j + 2
        if j > layers:
            return below, j - layers - 1
        return (side, 2) if j == layers else (tiles, j)

    @pl.loop(0, octants)
    def _(o):
        octant = first + o
        place = place_octant(octant)

        def emit(j, i, value):
            edge[outer[j], o, pl.ds(place[1][i], NY), :] = value

        advance(up, get, o, octant, place, co, tab, arg, keep, carry, emit)
        advance(down, get, o, octant, place, co, tab, arg.at[2:], keep.at[2:], carry, emit)
        for n in range(4):
            mom[flip(neg, 4, n)] += moments_of(edge[n, o], weight(tab, octant))


def middle_kernel(info, new, ma, mb, scale, *refs):
    tab = refs[0]
    newer, mom, _, arg, keep, carry = refs[1:]
    layers, octants = new.shape[0], new.shape[1]
    neg, first = info[0] != 0, info[1]
    js = list(range(2, layers - 1))
    co = {}
    for j in js:
        nat = flip(neg, layers, j)
        co[j] = coefficients(ma[nat] + mb[nat], scale[nat])
        mom[j - 2] = jnp.zeros((8, LANES), F32)
    prepare(js, co, tab, keep)

    @pl.loop(0, octants)
    def _(o):
        octant = first + o
        place = place_octant(octant)

        def emit(j, i, value):
            newer[j - 2, o, pl.ds(place[1][i], NY), :] = value

        advance(js, lambda j: (new, j), o, octant, place, co, tab, arg, keep, carry, emit)
        for j in js:
            mom[j - 2] += moments_of(newer[j - 2, o], weight(tab, octant))


def second_kernel(info, new, edge, ma, mb, middle, scale, *refs):
    tab = refs[0]
    newer, mom, _, arg, keep, carry = refs[1:]
    layers, octants = new.shape[0], new.shape[1]
    neg, first = info[0] != 0, info[1]
    up, down = [0, 1], [layers - 1]
    slots = {0: 0, 1: 1, layers - 1: 2}
    co = {}
    for j in slots:
        nat = flip(neg, layers, j)
        co[j] = coefficients(ma[nat] + mb[nat], scale[nat])
        mom[nat] = jnp.zeros((8, LANES), F32)
    for j in range(2, layers - 1):
        mom[flip(neg, layers, j)] = middle[j - 2]
    prepare(up + down, co, tab, keep)
    outer = {-2: 0, -1: 1, layers: 2}

    def get(j):
        return (edge, outer[j]) if j in outer else (new, j)

    @pl.loop(0, octants)
    def _(o):
        octant = first + o
        place = place_octant(octant)

        def emit(j, i, value):
            newer[slots[j], o, pl.ds(place[1][i], NY), :] = value

        advance(up, get, o, octant, place, co, tab, arg, keep, carry, emit)
        advance(down, get, o, octant, place, co, tab, arg.at[2:], keep.at[2:], carry, emit)
        for j, n in slots.items():
            mom[flip(neg, layers, j)] += moments_of(newer[n, o], weight(tab, octant))


def third_kernel(info, side, far, h3, edge, new, ma, mb, up_share, down_share, *refs):
    tab = refs[0]
    beside, tmp, arg, keep, carry, last, rim = refs[1:]
    layers, octants = new.shape[0], new.shape[1]
    neg, first = info[0] != 0, info[1]
    for i in range(2):
        convert(load_natural(h3, flip(neg, 2, i)), store_tile(last, i), tmp, octants)
    js, up, down = [-4, -3], [-2, -1], [layers]
    outer = {-2: 0, -1: 1, layers: 2, layers + 1: 3}
    co = {}
    for j in js:
        known = up_share[flip(neg, layers, layers + j)]
        co[j] = coefficients(known, known[5:6])
    for i, j in enumerate(up + down):
        slot = flip(neg, 4, i)
        beyond = up_share[flip(neg, layers, layers + j)] if j < 0 else down_share[flip(neg, layers, 0)]
        co[j] = coefficients(ma[slot] + mb[slot], beyond[5:6])
    prepare(js + up + down, co, tab, keep)

    def get0(j):
        return (last, j + 6) if j < -4 else (far, j + 4) if j < -2 else (side, j + 2)

    def get1(j):
        return (rim, j + 4) if j < -2 else (edge, outer[j]) if j in outer else (new, j)

    @pl.loop(0, octants)
    def _(o):
        octant = first + o
        place = place_octant(octant)

        def emit1(j, i, value):
            rim[j + 4, o, pl.ds(place[1][i], NY), :] = value

        def emit2(j, i, value):
            beside[outer[j], o, pl.ds(place[1][i], NY), :] = value

        advance(down, get1, o, octant, place, co, tab, arg.at[4:], keep.at[4:], carry, emit2)
        advance(js, get0, o, octant, place, co, tab, arg, keep, carry, emit1)
        advance(up, get1, o, octant, place, co, tab, arg.at[2:], keep.at[2:], carry, emit2)


def last_kernel(info, middle, newer, beside, ma, mb, scale, *refs):
    tab = refs[0]
    out, _, arg, keep, carry, result = refs[1:]
    layers, octants = out.shape[0], newer.shape[1]
    neg, first = info[0] != 0, info[1]
    js = list(range(layers))
    outer = {-2: 0, -1: 1, layers: 2}
    slots = {0: 0, 1: 1, layers - 1: 2}
    co = {}
    for j in js:
        nat = flip(neg, layers, j)
        co[j] = coefficients(ma[nat] + mb[nat], scale[nat])
    prepare(js, co, tab, keep)

    def get(j):
        if j in outer:
            return beside, outer[j]
        return (newer, slots[j]) if j in slots else (middle, j - 2)

    @pl.loop(0, octants)
    def _(o):
        octant = first + o
        place = place_octant(octant)
        starts = [place[1][i] // NY for i in range(NZ)]

        def emit(j, i, value):
            result[j, o, pl.ds(starts[i], NY, stride=NZ), :] = value

        advance(js, get, o, octant, place, co, tab, arg, keep, carry, emit)

    for j in js:
        nat = flip(neg, layers, j)
        for o in range(octants):
            out[nat, o * PER : (o + 1) * PER, :] = result[j, o].T[:PER]


def scratch(octants, layers, extra=()):
    square = (LANES, LANES)
    return [
        pltpu.VMEM((octants, *square), F32),
        pltpu.VMEM((layers, *square), F32),
        pltpu.VMEM((layers, *square), F32),
        pltpu.VMEM((3, *square), F32),
        *extra,
    ]


def run(body, args, outs, scratch_shapes, far_args=(), far_outs=()):
    call = pl.pallas_call(
        body,
        out_shape=[
            pltpu.HBM(shape, F32) if i in far_outs else jax.ShapeDtypeStruct(shape, F32)
            for i, shape in enumerate(outs)
        ],
        in_specs=[
            SMEM if a.dtype == jnp.int32 else HBM if i in far_args else VMEM for i, a in enumerate(args)
        ],
        out_specs=[HBM if i in far_outs else VMEM for i in range(len(outs))],
        scratch_shapes=scratch_shapes,
        compiler_params=pltpu.CompilerParams(vmem_limit_bytes=24 * 2**20),
    )
    args = [
        pltpu.with_memory_space_constraint(a, pltpu.HBM) if i in far_args else a
        for i, a in enumerate(args)
    ]
    return call(*args)


def exchange(part, axis):
    count = lax.axis_size(axis)
    if count == 1:
        return part, jnp.zeros_like(part)
    if count & (count - 1):
        return lax.psum(part, axis), jnp.zeros_like(part)
    bit = 1
    while True:
        other = lax.ppermute(part, axis, [(i, i ^ bit) for i in range(count)])
        bit *= 2
        if bit == count:
            return part, other
        part = part + other


def body(distribution, collision_scale):
    vel_count, layers, _ = distribution.shape
    oct_count, ring = lax.axis_size("oct"), lax.axis_size("space")
    octants = vel_count // PER
    assert vel_count % PER == 0 and oct_count % 2 == 0 and layers >= 6
    first = lax.axis_index("oct") * octants
    neg = first // 4 % 2
    info = jnp.stack([neg, first]).astype(jnp.int32)
    toward = []
    for o in range(oct_count):
        step = -1 if o * octants // 4 % 2 else 1
        for s in range(ring):
            toward.append((o * ring + s, o * ring + (s + step) % ring))
    against = [(target, source) for source, target in toward]

    def send(block, pairs):
        return lax.ppermute(block, ("oct", "space"), pairs)

    x = jnp.transpose(distribution, (1, 0, 2))
    tab = table()
    tile = (octants, LANES, LANES)
    rows = (8, LANES)
    block = (2, vel_count, LANES)
    two, six = pltpu.VMEM((2, *tile), F32), pltpu.VMEM((layers, *tile), F32)
    dma = pltpu.SemaphoreType.DMA
    h1, l1, x = run(
        cut_kernel,
        (info, x),
        [block, (1, vel_count, LANES), (layers, vel_count, LANES)],
        [dma((layers,)), dma((3,))],
        far_args=(1,),
        far_outs=(0, 1),
    )
    h1, l1 = send(h1, toward), send(l1, against)
    tiles, m0, scale, h2, h3, l2 = run(
        start_kernel,
        (info, x, collision_scale, tab),
        [(layers, *tile), (layers, *rows), (layers, 1, LANES), block, block, block],
        [pltpu.VMEM(tile, F32), dma((3,))],
        far_outs=(3, 4, 5),
    )
    m0 = exchange(m0, "oct")
    h2, h3, l2 = send(h2, toward), send(h3, toward), send(l2, against)
    (share,) = run(share_kernel, (*m0, scale), [(layers, *rows)], [])
    ch, cl = send(share, toward), send(share, against)
    new, side, m1 = run(
        first_kernel,
        (info, tiles, h1, l1, *m0, scale, tab),
        [(layers, *tile), (3, *tile), (layers, *rows)],
        scratch(octants, layers),
    )
    m1 = exchange(m1, "oct")
    edge, far, medge = run(
        edge_kernel,
        (info, tiles, side, h2, l2, ch, cl, tab),
        [(4, *tile), (2, *tile), (4, *rows)],
        scratch(octants, 4, [two]),
    )
    medge = exchange(medge, "oct")
    middle, mm = run(
        middle_kernel,
        (info, new, *m1, scale, tab),
        [(layers - 3, *tile), (layers - 3, *rows)],
        scratch(octants, layers - 3),
    )
    newer, m2 = run(
        second_kernel,
        (info, new, edge, *m1, mm, scale, tab),
        [(3, *tile), (layers, *rows)],
        scratch(octants, 3),
    )
    m2 = exchange(m2, "oct")
    (beside,) = run(
        third_kernel,
        (info, side, far, h3, edge, new, *medge, ch, cl, tab),
        [(3, *tile)],
        scratch(octants, 5, [two, two]),
    )
    (out,) = run(
        last_kernel,
        (info, middle, newer, beside, *m2, scale, tab),
        [(layers, vel_count, LANES)],
        scratch(octants, layers, [six]),
    )
    return jnp.transpose(out, (1, 0, 2))


def solution(mesh):
    return jax.shard_map(
        body,
        mesh=mesh,
        in_specs=(P("oct", "space", None), P(None, "space", None)),
        out_specs=P("oct", "space", None),
        check_vma=False,
    )
```

time: 66.8 us -> 67.7 us (1.013); the launches traced: 66.6 us -> 66.4 us
  Pallas kernels: 27.1 us -> 31.4 us
  local copies, waits for them, and re-layouts: 4.06 us -> 0.01 us
  waiting for transfers between devices: 11.2 us -> 9.32 us
  starting transfers between devices: 24 us -> 25.5 us
    pallas_call x6 -> x9, Pallas kernels: 27.1 us -> 31.4 us  [run(): return call(*args)]
    dynamic_slice x2 -> x0, local copies, waits for them, and re-layouts: 3.79 us -> none  [cut(): return lax.dynamic_slice_in_dim(x, start, count, 0)]
    ppermute x7, waiting for transfers between devices: 7.1 us -> 3.85 us  [send(): return lax.ppermute(block, ('oct', 'space'), pairs)]
    ppermute x3 -> x4, waiting for transfers between devices: 4.12 us -> 5.47 us  [exchange(): other = lax.ppermute(part, axis, [(i, i ^ bit) for i in range(count)])]
    ppermute x3 -> x4, starting transfers between devices: 7.74 us -> 8.75 us  [exchange(): other = lax.ppermute(part, axis, [(i, i ^ bit) for i in range(count)])]
  transfers between devices with their start and end apart: 10 -> 11, of which waited for: 4 -> 3; matrix products, arithmetic and copies ran while one was open for 2% -> 0% of each run, Pallas kernels for 30% -> 35%
where the time goes in v1:
time: 67.7 us; the launch traced here: 66.4 us
  Pallas kernels  31.4 us (46%)
  starting transfers between devices  25.5 us (38%)
  waiting for transfers between devices  9.32 us (14%)
    pallas_call x9, Pallas kernels, run(): return call(*args)  31.4 us
    ppermute x7, starting transfers between devices, send(): return lax.ppermute(block, ('oct', 'space'), pairs)  16.8 us
    ppermute x4, starting transfers between devices, exchange(): other = lax.ppermute(part, axis, [(i, i ^ bit) for i in range(count)])  8.75 us
    ppermute x4, waiting for transfers between devices, exchange(): other = lax.ppermute(part, axis, [(i, i ^ bit) for i in range(count)])  5.47 us
    ppermute x7, waiting for transfers between devices, send(): return lax.ppermute(block, ('oct', 'space'), pairs)  3.85 us
  transfers between devices with their start and end apart: 11, of which 3 were waited for; matrix products, arithmetic and copies ran while one was open for 0% of the time, Pallas kernels for 35%

profile of v1, /device:TPU:0, one launch (start us, length us, event | category | flops | bytes accessed | tf_op | source)
XLA Modules:
  0.0 66.4 jit_solution(5168198318170935605)
XLA Ops:
  0.0 0.1 pad_add_fusion.info
  0.1 2.5 %shard_map.37 = (f32[2,500,128]{2,1,0:T(8,128)}, f32[1,500,128]{2,1,0:T(8,128)}, f32[6,500,128]{2,1,0:T(8,128)S(1)}) custom-call(s32[2]{0:T(128)S(1)} %pad_add_fusion.info, f32[6,500,128]{2,1,0:T(8,128)} %bitcast.4), custom_call_target="tpu_custom_call" | custom-call | tf_op jit(solution)/shard_map/pallas_call | solution.py:493
  2.6 0.5 collective-permute-start
  3.2 2.7 %shard_map.38 = (f32[6,4,128,128]{3,2,1,0:T(8,128)S(1)}, f32[6,8,128]{2,1,0:T(8,128)S(1)}, f32[6,1,128]{2,1,0:T(1,128)S(1)}, f32[2,500,128]{2,1,0:T(8,128)}, f32...) custom-call(s32[2]{0:T(128)S(1)} %pad_add_fusion.info, f32[6,500,128]{2,1,0:T(8,128)S(1)} %get-tuple-element.24.x, ...), custom_call_target="tpu_custom_call" | custom-call | tf_op jit(solution)/shard_map/pallas_call | solution.py:493
  5.9 2.7 %collective-permute-start.4 = (f32[2,500,128]{2,1,0:T(8,128)}, f32[2,500,128]{2,1,0:T(8,128)S(1)}, u32[]{:S(2)}, u32[]{:S(2)}) collective-permute-start(f32[2,500,128]{2,1,0:T(8,128)} %get-tuple-element.34), channel_id=1, source_target_pairs={{0,1},{1,2},{2,3},{3,4},{4,5},{5,6},{6,7},{7,8},{8,9},{9,10},{10,1... | collective-permute-start | bytes 1536008 | tf_op jit(solution)/shard_map/ppermute | solution.py:527
  8.5 2.5 %collective-permute-start.5 = (f32[2,500,128]{2,1,0:T(8,128)}, f32[2,500,128]{2,1,0:T(8,128)S(1)}, u32[]{:S(2)}, u32[]{:S(2)}) collective-permute-start(f32[2,500,128]{2,1,0:T(8,128)} %get-tuple-element.35), channel_id=1, source_target_pairs={{1,0},{2,1},{3,2},{4,3},{5,4},{6,5},{7,6},{8,7},{9,8},{10,9},{11,1... | collective-permute-start | bytes 1536008 | tf_op jit(solution)/shard_map/ppermute | solution.py:527
  11.0 0.0 collective-permute-start.8
  11.0 6.5 %collective-permute-start.2 = (f32[6,8,128]{2,1,0:T(8,128)S(1)}, f32[6,8,128]{2,1,0:T(8,128)S(1)}, u32[]{:S(2)}, u32[]{:S(2)}) collective-permute-start(f32[6,8,128]{2,1,0:T(8,128)S(1)} %get-tuple-element.28.ma), channel_id=1, source_target_pairs={{0,16},{16,0},{1,17},{17,1},{2,18},{18,2},{3,19},{19,3},{4,20},{20... | collective-permute-start | bytes 73736 | tf_op jit(solution)/shard_map/ppermute | solution.py:504
  17.5 1.8 %collective-permute-done.2.mb = f32[6,8,128]{2,1,0:T(8,128)S(1)} collective-permute-done((f32[6,8,128]{2,1,0:T(8,128)S(1)}, f32[6,8,128]{2,1,0:T(8,128)S(1)}, u32[]{:S(2)}, u32[]{:S(2)}) %collective-permute-start.2) | collective-permute-done | bytes 24608 | tf_op jit(solution)/shard_map/ppermute | solution.py:504
  19.4 3.8 %collective-permute-done.1.l1 = f32[1,500,128]{2,1,0:T(8,128)S(1)} collective-permute-done((f32[1,500,128]{2,1,0:T(8,128)S(1)}, f32[1,500,128]{2,1,0:T(8,128)S(1)}, u32[]{:S(2)}, u32[]{:S(2)}) %collective-permute-start.1) | collective-permute-done | bytes 256032 | tf_op jit(solution)/shard_map/ppermute | solution.py:527
  23.2 4.7 %collective-permute-start.7 = (f32[6,8,128]{2,1,0:T(8,128)S(1)}, f32[6,8,128]{2,1,0:T(8,128)S(1)}, u32[]{:S(2)}, u32[]{:S(2)}) collective-permute-start(f32[6,8,128]{2,1,0:T(8,128)S(1)} %shard_map.41), channel_id=1, source_target_pairs={{1,0},{2,1},{3,2},{4,3},{5,4},{6,5},{7,6},{8,7},{9,8},{10,9},{11,1... | collective-permute-start | bytes 73736 | tf_op jit(solution)/shard_map/ppermute | solution.py:527
  27.9 0.0 collective-permute-done.h1
  27.9 6.4 %collective-permute-start.6 = (f32[6,8,128]{2,1,0:T(8,128)S(1)}, f32[6,8,128]{2,1,0:T(8,128)S(1)}, u32[]{:S(2)}, u32[]{:S(2)}) collective-permute-start(f32[6,8,128]{2,1,0:T(8,128)S(1)} %shard_map.41), channel_id=1, source_target_pairs={{0,1},{1,2},{2,3},{3,4},{4,5},{5,6},{6,7},{7,8},{8,9},{9,10},{10,1... | collective-permute-start | bytes 73736 | tf_op jit(solution)/shard_map/ppermute | solution.py:527
  34.3 5.4 %shard_map.39 = (f32[6,4,128,128]{3,2,1,0:T(8,128)S(1)}, f32[3,4,128,128]{3,2,1,0:T(8,128)S(1)}, f32[6,8,128]{2,1,0:T(8,128)S(1)}) custom-call(s32[2]{0:T(128)S(1)} %pad_add_fusion.info, f32[6,4,128,128]{3,2,1,0:T(8,128)S(1)} %get-tuple-element.25.tiles, f32[2,500,128]{2,1,0:T(8,128)S(1)} %collective-permute-done.h1, ...), custom_call_target="tpu_custom_call" | custom-call | tf_op jit(solution)/shard_map/pallas_call | solution.py:493
  39.7 0.0 collective-permute-done.7.down_share
  39.7 0.1 collective-permute-start.3
  39.9 4.3 %shard_map.42 = (f32[4,4,128,128]{3,2,1,0:T(8,128)S(1)}, f32[2,4,128,128]{3,2,1,0:T(8,128)S(1)}, f32[4,8,128]{2,1,0:T(8,128)S(1)}) custom-call(s32[2]{0:T(128)S(1)} %pad_add_fusion.info, f32[6,4,128,128]{3,2,1,0:T(8,128)S(1)} %get-tuple-element.25.tiles, f32[3,4,128,128]{3,2,1,0:T(8,128)S(1)} %get-tuple-element.33.side, ...), custom_call_target="tpu_custom_call" | custom-call | tf_op jit(solution)/shard_map/pallas_call | solution.py:493
  44.2 3.4 %shard_map.40 = (f32[3,4,128,128]{3,2,1,0:T(8,128)S(1)}, f32[3,8,128]{2,1,0:T(8,128)S(1)}) custom-call(s32[2]{0:T(128)S(1)} %pad_add_fusion.info, f32[6,4,128,128]{3,2,1,0:T(8,128)S(1)} %get-tuple-element.30.new, f32[6,8,128]{2,1,0:T(8,128)S(1)} %get-tuple-element.31.ma, f32[6,8,128]{2,1,0:T(8,128)S(1)} %collective-permute-done.3.mb, ...), custom_call_target="tpu_custom_call" | custom-call | tf_op jit(solution)/shard_map/pallas_call | solution.py:493
  47.7 3.5 %shard_map.43 = (f32[3,4,128,128]{3,2,1,0:T(8,128)S(1)}, f32[6,8,128]{2,1,0:T(8,128)S(1)}) custom-call(s32[2]{0:T(128)S(1)} %pad_add_fusion.info, f32[6,4,128,128]{3,2,1,0:T(8,128)S(1)} %get-tuple-element.30.new, f32[4,4,128,128]{3,2,1,0:T(8,128)S(1)} %get-tuple-element.36.edge, f32[6,8,128]{2,1,0:T(8,128)S(1)} %get-tuple-element.31.ma, ...), custom_call_target="tpu_custom_call" | custom-call | tf_op jit(solution)/shard_map/pallas_call | solution.py:493
  51.2 2.0 %collective-permute-start.10 = (f32[6,8,128]{2,1,0:T(8,128)S(1)}, f32[6,8,128]{2,1,0:T(8,128)S(1)}, u32[]{:S(2)}, u32[]{:S(2)}) collective-permute-start(f32[6,8,128]{2,1,0:T(8,128)S(1)} %get-tuple-element.42.ma), channel_id=1, source_target_pairs={{0,16},{16,0},{1,17},{17,1},{2,18},{18,2},{3,19},{19,3},{4,20},{20... | collective-permute-start | bytes 73736 | tf_op jit(solution)/shard_map/ppermute | solution.py:504
  53.2 0.1 collective-permute-start.9
  53.3 3.7 %collective-permute-done.9.mb = f32[4,8,128]{2,1,0:T(8,128)S(1)} collective-permute-done((f32[4,8,128]{2,1,0:T(8,128)S(1)}, f32[4,8,128]{2,1,0:T(8,128)S(1)}, u32[]{:S(2)}, u32[]{:S(2)}) %collective-permute-start.9) | collective-permute-done | bytes 16416 | tf_op jit(solution)/shard_map/ppermute | solution.py:504
  56.9 3.8 %shard_map.44.beside = f32[3,4,128,128]{3,2,1,0:T(8,128)S(1)} custom-call(s32[2]{0:T(128)S(1)} %pad_add_fusion.info, f32[3,4,128,128]{3,2,1,0:T(8,128)S(1)} %get-tuple-element.33.side, f32[2,4,128,128]{3,2,1,0:T(8,128)S(1)} %get-tuple-element.39.far, f32[2,500,128]{2,1,0:T(8,128)S(1)} %collective-permute-done.8.h3, ...), custom_call_target="tpu_custom_call" | custom-call | tf_op jit(solution)/shard_map/pallas_call | solution.py:493
  60.8 5.6 %shard_map.45 = f32[6,500,128]{2,1,0:T(8,128)} custom-call(s32[2]{0:T(128)S(1)} %pad_add_fusion.info, f32[3,4,128,128]{3,2,1,0:T(8,128)S(1)} %get-tuple-element.32.middle, f32[3,4,128,128]{3,2,1,0:T(8,128)S(1)} %get-tuple-element.38.newer, f32[3,4,128,128]{3,2,1,0:T(8,128)S(1)} %shard_map.44.beside, f32[6,8,128]{2,1,0:T(8,128)S(1)} %get-tuple-element.42.ma, ...), custom_call_target="tpu_custom_call" | custom-call | tf_op jit(solution)/shard_map/pallas_call | solution.py:493
  (15 shorter events, 0.0 us)
Async XLA Ops:
  0.0 3.2 %copy-start = (bf16[9,48,128]{2,1,0:T(8,128)(2,1)S(1)}, bf16[9,48,128]{2,1,0:T(8,128)(2,1)}, u32[]{:S(2)}) copy-start(bf16[9,48,128]{2,1,0:T(8,128)(2,1)} %constant.35.clone.tab.refs_0_) | copy-start | bytes 331780
  0.0 3.1 %copy-start.1 = (f32[1,6,128]{2,0,1:T(1,128)S(1)}, f32[1,6,128]{2,0,1:T(1,128)}, u32[]{:S(2)}) copy-start(f32[1,6,128]{2,0,1:T(1,128)} %param.4) | copy-start | bytes 9220
  2.6 16.7 %copy-start.2 = (f32[1,500,128]{2,1,0:T(8,128)S(1)}, f32[1,500,128]{2,1,0:T(8,128)}, u32[]{:S(2)}) copy-start(f32[1,500,128]{2,1,0:T(8,128)} %get-tuple-element.27) | copy-start | bytes 768004
  2.6 25.3 %collective-permute-start = (f32[2,500,128]{2,1,0:T(8,128)}, f32[2,500,128]{2,1,0:T(8,128)S(1)}, u32[]{:S(2)}, u32[]{:S(2)}) collective-permute-start(f32[2,500,128]{2,1,0:T(8,128)} %get-tuple-element.26), channel_id=1, source_target_pairs={{0,1},{1,2},{2,3},{3,4},{4,5},{5,6},{6,7},{7,8},{8,9},{9,10},{10,1... | collective-permute-start | bytes 1536008 | tf_op jit(solution)/shard_map/ppermute | solution.py:527
  5.9 34.0 %collective-permute-start.4 = (f32[2,500,128]{2,1,0:T(8,128)}, f32[2,500,128]{2,1,0:T(8,128)S(1)}, u32[]{:S(2)}, u32[]{:S(2)}) collective-permute-start(f32[2,500,128]{2,1,0:T(8,128)} %get-tuple-element.34), channel_id=1, source_target_pairs={{0,1},{1,2},{2,3},{3,4},{4,5},{5,6},{6,7},{7,8},{8,9},{9,10},{10,1... | collective-permute-start | bytes 1536008 | tf_op jit(solution)/shard_map/ppermute | solution.py:527
  8.5 31.3 %collective-permute-start.5 = (f32[2,500,128]{2,1,0:T(8,128)}, f32[2,500,128]{2,1,0:T(8,128)S(1)}, u32[]{:S(2)}, u32[]{:S(2)}) collective-permute-start(f32[2,500,128]{2,1,0:T(8,128)} %get-tuple-element.35), channel_id=1, source_target_pairs={{1,0},{2,1},{3,2},{4,3},{5,4},{6,5},{7,6},{8,7},{9,8},{10,9},{11,1... | collective-permute-start | bytes 1536008 | tf_op jit(solution)/shard_map/ppermute | solution.py:527
  11.0 42.2 %collective-permute-start.8 = (f32[2,500,128]{2,1,0:T(8,128)}, f32[2,500,128]{2,1,0:T(8,128)S(1)}, u32[]{:S(2)}, u32[]{:S(2)}) collective-permute-start(f32[2,500,128]{2,1,0:T(8,128)} %get-tuple-element.40), channel_id=1, source_target_pairs={{0,1},{1,2},{2,3},{3,4},{4,5},{5,6},{6,7},{7,8},{8,9},{9,10},{10,1... | collective-permute-start | bytes 1536008 | tf_op jit(solution)/shard_map/ppermute | solution.py:527
  11.0 8.3 %collective-permute-start.2 = (f32[6,8,128]{2,1,0:T(8,128)S(1)}, f32[6,8,128]{2,1,0:T(8,128)S(1)}, u32[]{:S(2)}, u32[]{:S(2)}) collective-permute-start(f32[6,8,128]{2,1,0:T(8,128)S(1)} %get-tuple-element.28.ma), channel_id=1, source_target_pairs={{0,16},{16,0},{1,17},{17,1},{2,18},{18,2},{3,19},{19,3},{4,20},{20... | collective-permute-start | bytes 73736 | tf_op jit(solution)/shard_map/ppermute | solution.py:504
  19.3 3.9 %collective-permute-start.1 = (f32[1,500,128]{2,1,0:T(8,128)S(1)}, f32[1,500,128]{2,1,0:T(8,128)S(1)}, u32[]{:S(2)}, u32[]{:S(2)}) collective-permute-start(f32[1,500,128]{2,1,0:T(8,128)S(1)} %copy-done.2), channel_id=1, source_target_pairs={{1,0},{2,1},{3,2},{4,3},{5,4},{6,5},{7,6},{8,7},{9,8},{10,9},{11,1... | collective-permute-start | bytes 768008 | tf_op jit(solution)/shard_map/ppermute | solution.py:527
  23.2 16.5 %collective-permute-start.7 = (f32[6,8,128]{2,1,0:T(8,128)S(1)}, f32[6,8,128]{2,1,0:T(8,128)S(1)}, u32[]{:S(2)}, u32[]{:S(2)}) collective-permute-start(f32[6,8,128]{2,1,0:T(8,128)S(1)} %shard_map.41), channel_id=1, source_target_pairs={{1,0},{2,1},{3,2},{4,3},{5,4},{6,5},{7,6},{8,7},{9,8},{10,9},{11,1... | collective-permute-start | bytes 73736 | tf_op jit(solution)/shard_map/ppermute | solution.py:527
  27.9 12.0 %collective-permute-start.6 = (f32[6,8,128]{2,1,0:T(8,128)S(1)}, f32[6,8,128]{2,1,0:T(8,128)S(1)}, u32[]{:S(2)}, u32[]{:S(2)}) collective-permute-start(f32[6,8,128]{2,1,0:T(8,128)S(1)} %shard_map.41), channel_id=1, source_target_pairs={{0,1},{1,2},{2,3},{3,4},{4,5},{5,6},{6,7},{7,8},{8,9},{9,10},{10,1... | collective-permute-start | bytes 73736 | tf_op jit(solution)/shard_map/ppermute | solution.py:527
  39.7 4.5 %collective-permute-start.3 = (f32[6,8,128]{2,1,0:T(8,128)S(1)}, f32[6,8,128]{2,1,0:T(8,128)S(1)}, u32[]{:S(2)}, u32[]{:S(2)}) collective-permute-start(f32[6,8,128]{2,1,0:T(8,128)S(1)} %get-tuple-element.31.ma), channel_id=1, source_target_pairs={{0,16},{16,0},{1,17},{17,1},{2,18},{18,2},{3,19},{19,3},{4,20},{20... | collective-permute-start | bytes 73736 | tf_op jit(solution)/shard_map/ppermute | solution.py:504
  51.2 9.6 %collective-permute-start.10 = (f32[6,8,128]{2,1,0:T(8,128)S(1)}, f32[6,8,128]{2,1,0:T(8,128)S(1)}, u32[]{:S(2)}, u32[]{:S(2)}) collective-permute-start(f32[6,8,128]{2,1,0:T(8,128)S(1)} %get-tuple-element.42.ma), channel_id=1, source_target_pairs={{0,16},{16,0},{1,17},{17,1},{2,18},{18,2},{3,19},{19,3},{4,20},{20... | collective-permute-start | bytes 73736 | tf_op jit(solution)/shard_map/ppermute | solution.py:504
  53.2 3.7 %collective-permute-start.9 = (f32[4,8,128]{2,1,0:T(8,128)S(1)}, f32[4,8,128]{2,1,0:T(8,128)S(1)}, u32[]{:S(2)}, u32[]{:S(2)}) collective-permute-start(f32[4,8,128]{2,1,0:T(8,128)S(1)} %get-tuple-element.41.ma), channel_id=1, source_target_pairs={{0,16},{16,0},{1,17},{17,1},{2,18},{18,2},{3,19},{19,3},{4,20},{20... | collective-permute-start | bytes 49160 | tf_op jit(solution)/shard_map/ppermute | solution.py:504

commit v2 on v1

--- a/solution.py
+++ b/solution.py
@@ -225,9 +225,14 @@
     ]
     for c in copies:
         c.start()
+
+    @pl.loop(0, layers)
+    def _(j):
+        nat = flip(neg, layers, j)
+        convert(load_natural(x, nat), store_tile(tiles, j), tmp, octants)
+
     for j in range(layers):
         nat = flip(neg, layers, j)
-        convert(load_natural(x, nat), store_tile(tiles, j), tmp, octants)
         total = 0.0
         for o in range(octants):
             total = total + moments_of(tiles[j, o], weight(tab, first + o))
@@ -427,7 +432,7 @@
 
 def last_kernel(info, middle, newer, beside, ma, mb, scale, *refs):
     tab = refs[0]
-    out, _, arg, keep, carry, result = refs[1:]
+    out, _, arg, keep, carry, result, ready, sems = refs[1:]
     layers, octants = out.shape[0], newer.shape[1]
     neg, first = info[0] != 0, info[1]
     js = list(range(layers))
@@ -455,10 +460,14 @@
 
         advance(js, get, o, octant, place, co, tab, arg, keep, carry, emit)
 
+    copies = []
     for j in js:
-        nat = flip(neg, layers, j)
         for o in range(octants):
-            out[nat, o * PER : (o + 1) * PER, :] = result[j, o].T[:PER]
+            ready[j, o * PER : (o + 1) * PER, :] = result[j, o].T[:PER]
+        copies.append(pltpu.make_async_copy(ready.at[j], out.at[flip(neg, layers, j)], sems.at[j]))
+        copies[j].start()
+    for c in copies:
+        c.wait()
 
 
 def scratch(octants, layers, extra=()):
@@ -590,7 +599,10 @@
         last_kernel,
         (info, middle, newer, beside, *m2, scale, tab),
         [(layers, vel_count, LANES)],
-        scratch(octants, layers, [six]),
+        scratch(
+            octants, layers, [six, pltpu.VMEM((layers, vel_count, LANES), F32), dma((layers,))]
+        ),
+        far_outs=(0,),
     )
     return jnp.transpose(out, (1, 0, 2))
 

time: 67.7 us -> 67.4 us (level)
  no operation moved by 1% of the time
where the time goes in v2:
time: 67.4 us; the launch traced here: 66.1 us
  Pallas kernels  30.9 us (46%)
  starting transfers between devices  25.6 us (38%)
  waiting for transfers between devices  9.32 us (14%)
    pallas_call x9, Pallas kernels, run(): return call(*args)  30.9 us
    ppermute x7, starting transfers between devices, send(): return lax.ppermute(block, ('oct', 'space'), pairs)  16.9 us
    ppermute x4, starting transfers between devices, exchange(): other = lax.ppermute(part, axis, [(i, i ^ bit) for i in range(count)])  8.71 us
    ppermute x4, waiting for transfers between devices, exchange(): other = lax.ppermute(part, axis, [(i, i ^ bit) for i in range(count)])  5.47 us
    ppermute x7, waiting for transfers between devices, send(): return lax.ppermute(block, ('oct', 'space'), pairs)  3.85 us
  transfers between devices with their start and end apart: 11, of which 3 were waited for; matrix products, arithmetic and copies ran while one was open for 0% of the time, Pallas kernels for 35%

profile of v2, /device:TPU:0, one launch (start us, length us, event | category | flops | bytes accessed | tf_op | source)
XLA Modules:
  0.0 66.1 jit_solution(3549979459053400395)
XLA Ops:
  0.0 0.1 pad_add_fusion.info
  0.1 2.5 %shard_map.37 = (f32[2,500,128]{2,1,0:T(8,128)}, f32[1,500,128]{2,1,0:T(8,128)}, f32[6,500,128]{2,1,0:T(8,128)S(1)}) custom-call(s32[2]{0:T(128)S(1)} %pad_add_fusion.info, f32[6,500,128]{2,1,0:T(8,128)} %bitcast.4), custom_call_target="tpu_custom_call" | custom-call | tf_op jit(solution)/shard_map/pallas_call | solution.py:502
  2.6 0.5 collective-permute-start
  3.2 2.6 %shard_map.38 = (f32[6,4,128,128]{3,2,1,0:T(8,128)S(1)}, f32[6,8,128]{2,1,0:T(8,128)S(1)}, f32[6,1,128]{2,1,0:T(1,128)S(1)}, f32[2,500,128]{2,1,0:T(8,128)}, f32...) custom-call(s32[2]{0:T(128)S(1)} %pad_add_fusion.info, f32[6,500,128]{2,1,0:T(8,128)S(1)} %get-tuple-element.24.x, ...), custom_call_target="tpu_custom_call" | custom-call | tf_op jit(solution)/shard_map/pallas_call | solution.py:502
  5.7 2.7 %collective-permute-start.4 = (f32[2,500,128]{2,1,0:T(8,128)}, f32[2,500,128]{2,1,0:T(8,128)S(1)}, u32[]{:S(2)}, u32[]{:S(2)}) collective-permute-start(f32[2,500,128]{2,1,0:T(8,128)} %get-tuple-element.34), channel_id=1, source_target_pairs={{0,1},{1,2},{2,3},{3,4},{4,5},{5,6},{6,7},{7,8},{8,9},{9,10},{10,1... | collective-permute-start | bytes 1536008 | tf_op jit(solution)/shard_map/ppermute | solution.py:536
  8.4 2.5 %collective-permute-start.5 = (f32[2,500,128]{2,1,0:T(8,128)}, f32[2,500,128]{2,1,0:T(8,128)S(1)}, u32[]{:S(2)}, u32[]{:S(2)}) collective-permute-start(f32[2,500,128]{2,1,0:T(8,128)} %get-tuple-element.35), channel_id=1, source_target_pairs={{1,0},{2,1},{3,2},{4,3},{5,4},{6,5},{7,6},{8,7},{9,8},{10,9},{11,1... | collective-permute-start | bytes 1536008 | tf_op jit(solution)/shard_map/ppermute | solution.py:536
  10.9 0.0 collective-permute-start.8
  10.9 6.5 %collective-permute-start.2 = (f32[6,8,128]{2,1,0:T(8,128)S(1)}, f32[6,8,128]{2,1,0:T(8,128)S(1)}, u32[]{:S(2)}, u32[]{:S(2)}) collective-permute-start(f32[6,8,128]{2,1,0:T(8,128)S(1)} %get-tuple-element.28.ma), channel_id=1, source_target_pairs={{0,16},{16,0},{1,17},{17,1},{2,18},{18,2},{3,19},{19,3},{4,20},{20... | collective-permute-start | bytes 73736 | tf_op jit(solution)/shard_map/ppermute | solution.py:513
  17.4 1.8 %collective-permute-done.2.mb = f32[6,8,128]{2,1,0:T(8,128)S(1)} collective-permute-done((f32[6,8,128]{2,1,0:T(8,128)S(1)}, f32[6,8,128]{2,1,0:T(8,128)S(1)}, u32[]{:S(2)}, u32[]{:S(2)}) %collective-permute-start.2) | collective-permute-done | bytes 24608 | tf_op jit(solution)/shard_map/ppermute | solution.py:513
  19.2 3.8 %collective-permute-done.1.l1 = f32[1,500,128]{2,1,0:T(8,128)S(1)} collective-permute-done((f32[1,500,128]{2,1,0:T(8,128)S(1)}, f32[1,500,128]{2,1,0:T(8,128)S(1)}, u32[]{:S(2)}, u32[]{:S(2)}) %collective-permute-start.1) | collective-permute-done | bytes 256032 | tf_op jit(solution)/shard_map/ppermute | solution.py:536
  23.0 4.7 %collective-permute-start.7 = (f32[6,8,128]{2,1,0:T(8,128)S(1)}, f32[6,8,128]{2,1,0:T(8,128)S(1)}, u32[]{:S(2)}, u32[]{:S(2)}) collective-permute-start(f32[6,8,128]{2,1,0:T(8,128)S(1)} %shard_map.41), channel_id=1, source_target_pairs={{1,0},{2,1},{3,2},{4,3},{5,4},{6,5},{7,6},{8,7},{9,8},{10,9},{11,1... | collective-permute-start | bytes 73736 | tf_op jit(solution)/shard_map/ppermute | solution.py:536
  27.8 0.0 collective-permute-done.h1
  27.8 6.5 %collective-permute-start.6 = (f32[6,8,128]{2,1,0:T(8,128)S(1)}, f32[6,8,128]{2,1,0:T(8,128)S(1)}, u32[]{:S(2)}, u32[]{:S(2)}) collective-permute-start(f32[6,8,128]{2,1,0:T(8,128)S(1)} %shard_map.41), channel_id=1, source_target_pairs={{0,1},{1,2},{2,3},{3,4},{4,5},{5,6},{6,7},{7,8},{8,9},{9,10},{10,1... | collective-permute-start | bytes 73736 | tf_op jit(solution)/shard_map/ppermute | solution.py:536
  34.3 5.4 %shard_map.39 = (f32[6,4,128,128]{3,2,1,0:T(8,128)S(1)}, f32[3,4,128,128]{3,2,1,0:T(8,128)S(1)}, f32[6,8,128]{2,1,0:T(8,128)S(1)}) custom-call(s32[2]{0:T(128)S(1)} %pad_add_fusion.info, f32[6,4,128,128]{3,2,1,0:T(8,128)S(1)} %get-tuple-element.25.tiles, f32[2,500,128]{2,1,0:T(8,128)S(1)} %collective-permute-done.h1, ...), custom_call_target="tpu_custom_call" | custom-call | tf_op jit(solution)/shard_map/pallas_call | solution.py:502
  39.7 0.0 collective-permute-done.7.down_share
  39.7 0.1 collective-permute-start.3
  39.8 4.3 %shard_map.42 = (f32[4,4,128,128]{3,2,1,0:T(8,128)S(1)}, f32[2,4,128,128]{3,2,1,0:T(8,128)S(1)}, f32[4,8,128]{2,1,0:T(8,128)S(1)}) custom-call(s32[2]{0:T(128)S(1)} %pad_add_fusion.info, f32[6,4,128,128]{3,2,1,0:T(8,128)S(1)} %get-tuple-element.25.tiles, f32[3,4,128,128]{3,2,1,0:T(8,128)S(1)} %get-tuple-element.33.side, ...), custom_call_target="tpu_custom_call" | custom-call | tf_op jit(solution)/shard_map/pallas_call | solution.py:502
  44.2 3.5 %shard_map.40 = (f32[3,4,128,128]{3,2,1,0:T(8,128)S(1)}, f32[3,8,128]{2,1,0:T(8,128)S(1)}) custom-call(s32[2]{0:T(128)S(1)} %pad_add_fusion.info, f32[6,4,128,128]{3,2,1,0:T(8,128)S(1)} %get-tuple-element.30.new, f32[6,8,128]{2,1,0:T(8,128)S(1)} %get-tuple-element.31.ma, f32[6,8,128]{2,1,0:T(8,128)S(1)} %collective-permute-done.3.mb, ...), custom_call_target="tpu_custom_call" | custom-call | tf_op jit(solution)/shard_map/pallas_call | solution.py:502
  47.6 3.5 %shard_map.43 = (f32[3,4,128,128]{3,2,1,0:T(8,128)S(1)}, f32[6,8,128]{2,1,0:T(8,128)S(1)}) custom-call(s32[2]{0:T(128)S(1)} %pad_add_fusion.info, f32[6,4,128,128]{3,2,1,0:T(8,128)S(1)} %get-tuple-element.30.new, f32[4,4,128,128]{3,2,1,0:T(8,128)S(1)} %get-tuple-element.36.edge, f32[6,8,128]{2,1,0:T(8,128)S(1)} %get-tuple-element.31.ma, ...), custom_call_target="tpu_custom_call" | custom-call | tf_op jit(solution)/shard_map/pallas_call | solution.py:502
  51.1 2.1 %collective-permute-start.10 = (f32[6,8,128]{2,1,0:T(8,128)S(1)}, f32[6,8,128]{2,1,0:T(8,128)S(1)}, u32[]{:S(2)}, u32[]{:S(2)}) collective-permute-start(f32[6,8,128]{2,1,0:T(8,128)S(1)} %get-tuple-element.42.ma), channel_id=1, source_target_pairs={{0,16},{16,0},{1,17},{17,1},{2,18},{18,2},{3,19},{19,3},{4,20},{20... | collective-permute-start | bytes 73736 | tf_op jit(solution)/shard_map/ppermute | solution.py:513
  53.2 0.1 collective-permute-start.9
  53.3 3.7 %collective-permute-done.9.mb = f32[4,8,128]{2,1,0:T(8,128)S(1)} collective-permute-done((f32[4,8,128]{2,1,0:T(8,128)S(1)}, f32[4,8,128]{2,1,0:T(8,128)S(1)}, u32[]{:S(2)}, u32[]{:S(2)}) %collective-permute-start.9) | collective-permute-done | bytes 16416 | tf_op jit(solution)/shard_map/ppermute | solution.py:513
  56.9 3.8 %shard_map.44.beside = f32[3,4,128,128]{3,2,1,0:T(8,128)S(1)} custom-call(s32[2]{0:T(128)S(1)} %pad_add_fusion.info, f32[3,4,128,128]{3,2,1,0:T(8,128)S(1)} %get-tuple-element.33.side, f32[2,4,128,128]{3,2,1,0:T(8,128)S(1)} %get-tuple-element.39.far, f32[2,500,128]{2,1,0:T(8,128)S(1)} %collective-permute-done.8.h3, ...), custom_call_target="tpu_custom_call" | custom-call | tf_op jit(solution)/shard_map/pallas_call | solution.py:502
  60.8 5.3 %shard_map.45 = f32[6,500,128]{2,1,0:T(8,128)} custom-call(s32[2]{0:T(128)S(1)} %pad_add_fusion.info, f32[3,4,128,128]{3,2,1,0:T(8,128)S(1)} %get-tuple-element.32.middle, f32[3,4,128,128]{3,2,1,0:T(8,128)S(1)} %get-tuple-element.38.newer, f32[3,4,128,128]{3,2,1,0:T(8,128)S(1)} %shard_map.44.beside, f32[6,8,128]{2,1,0:T(8,128)S(1)} %get-tuple-element.42.ma, ...), custom_call_target="tpu_custom_call" | custom-call | tf_op jit(solution)/shard_map/pallas_call | solution.py:502
  (15 shorter events, 0.0 us)
Async XLA Ops:
  0.0 3.2 %copy-start = (bf16[9,48,128]{2,1,0:T(8,128)(2,1)S(1)}, bf16[9,48,128]{2,1,0:T(8,128)(2,1)}, u32[]{:S(2)}) copy-start(bf16[9,48,128]{2,1,0:T(8,128)(2,1)} %constant.35.clone.tab.refs_0_) | copy-start | bytes 331780
  0.0 3.1 %copy-start.1 = (f32[1,6,128]{2,0,1:T(1,128)S(1)}, f32[1,6,128]{2,0,1:T(1,128)}, u32[]{:S(2)}) copy-start(f32[1,6,128]{2,0,1:T(1,128)} %param.4) | copy-start | bytes 9220
  2.6 16.6 %copy-start.2 = (f32[1,500,128]{2,1,0:T(8,128)S(1)}, f32[1,500,128]{2,1,0:T(8,128)}, u32[]{:S(2)}) copy-start(f32[1,500,128]{2,1,0:T(8,128)} %get-tuple-element.27) | copy-start | bytes 768004
  2.6 25.1 %collective-permute-start = (f32[2,500,128]{2,1,0:T(8,128)}, f32[2,500,128]{2,1,0:T(8,128)S(1)}, u32[]{:S(2)}, u32[]{:S(2)}) collective-permute-start(f32[2,500,128]{2,1,0:T(8,128)} %get-tuple-element.26), channel_id=1, source_target_pairs={{0,1},{1,2},{2,3},{3,4},{4,5},{5,6},{6,7},{7,8},{8,9},{9,10},{10,1... | collective-permute-start | bytes 1536008 | tf_op jit(solution)/shard_map/ppermute | solution.py:536
  5.7 34.1 %collective-permute-start.4 = (f32[2,500,128]{2,1,0:T(8,128)}, f32[2,500,128]{2,1,0:T(8,128)S(1)}, u32[]{:S(2)}, u32[]{:S(2)}) collective-permute-start(f32[2,500,128]{2,1,0:T(8,128)} %get-tuple-element.34), channel_id=1, source_target_pairs={{0,1},{1,2},{2,3},{3,4},{4,5},{5,6},{6,7},{7,8},{8,9},{9,10},{10,1... | collective-permute-start | bytes 1536008 | tf_op jit(solution)/shard_map/ppermute | solution.py:536
  8.4 31.4 %collective-permute-start.5 = (f32[2,500,128]{2,1,0:T(8,128)}, f32[2,500,128]{2,1,0:T(8,128)S(1)}, u32[]{:S(2)}, u32[]{:S(2)}) collective-permute-start(f32[2,500,128]{2,1,0:T(8,128)} %get-tuple-element.35), channel_id=1, source_target_pairs={{1,0},{2,1},{3,2},{4,3},{5,4},{6,5},{7,6},{8,7},{9,8},{10,9},{11,1... | collective-permute-start | bytes 1536008 | tf_op jit(solution)/shard_map/ppermute | solution.py:536
  10.9 42.4 %collective-permute-start.8 = (f32[2,500,128]{2,1,0:T(8,128)}, f32[2,500,128]{2,1,0:T(8,128)S(1)}, u32[]{:S(2)}, u32[]{:S(2)}) collective-permute-start(f32[2,500,128]{2,1,0:T(8,128)} %get-tuple-element.40), channel_id=1, source_target_pairs={{0,1},{1,2},{2,3},{3,4},{4,5},{5,6},{6,7},{7,8},{8,9},{9,10},{10,1... | collective-permute-start | bytes 1536008 | tf_op jit(solution)/shard_map/ppermute | solution.py:536
  10.9 8.3 %collective-permute-start.2 = (f32[6,8,128]{2,1,0:T(8,128)S(1)}, f32[6,8,128]{2,1,0:T(8,128)S(1)}, u32[]{:S(2)}, u32[]{:S(2)}) collective-permute-start(f32[6,8,128]{2,1,0:T(8,128)S(1)} %get-tuple-element.28.ma), channel_id=1, source_target_pairs={{0,16},{16,0},{1,17},{17,1},{2,18},{18,2},{3,19},{19,3},{4,20},{20... | collective-permute-start | bytes 73736 | tf_op jit(solution)/shard_map/ppermute | solution.py:513
  19.2 3.9 %collective-permute-start.1 = (f32[1,500,128]{2,1,0:T(8,128)S(1)}, f32[1,500,128]{2,1,0:T(8,128)S(1)}, u32[]{:S(2)}, u32[]{:S(2)}) collective-permute-start(f32[1,500,128]{2,1,0:T(8,128)S(1)} %copy-done.2), channel_id=1, source_target_pairs={{1,0},{2,1},{3,2},{4,3},{5,4},{6,5},{7,6},{8,7},{9,8},{10,9},{11,1... | collective-permute-start | bytes 768008 | tf_op jit(solution)/shard_map/ppermute | solution.py:536
  23.0 16.7 %collective-permute-start.7 = (f32[6,8,128]{2,1,0:T(8,128)S(1)}, f32[6,8,128]{2,1,0:T(8,128)S(1)}, u32[]{:S(2)}, u32[]{:S(2)}) collective-permute-start(f32[6,8,128]{2,1,0:T(8,128)S(1)} %shard_map.41), channel_id=1, source_target_pairs={{1,0},{2,1},{3,2},{4,3},{5,4},{6,5},{7,6},{8,7},{9,8},{10,9},{11,1... | collective-permute-start | bytes 73736 | tf_op jit(solution)/shard_map/ppermute | solution.py:536
  27.8 12.0 %collective-permute-start.6 = (f32[6,8,128]{2,1,0:T(8,128)S(1)}, f32[6,8,128]{2,1,0:T(8,128)S(1)}, u32[]{:S(2)}, u32[]{:S(2)}) collective-permute-start(f32[6,8,128]{2,1,0:T(8,128)S(1)} %shard_map.41), channel_id=1, source_target_pairs={{0,1},{1,2},{2,3},{3,4},{4,5},{5,6},{6,7},{7,8},{8,9},{9,10},{10,1... | collective-permute-start | bytes 73736 | tf_op jit(solution)/shard_map/ppermute | solution.py:536
  39.7 4.5 %collective-permute-start.3 = (f32[6,8,128]{2,1,0:T(8,128)S(1)}, f32[6,8,128]{2,1,0:T(8,128)S(1)}, u32[]{:S(2)}, u32[]{:S(2)}) collective-permute-start(f32[6,8,128]{2,1,0:T(8,128)S(1)} %get-tuple-element.31.ma), channel_id=1, source_target_pairs={{0,16},{16,0},{1,17},{17,1},{2,18},{18,2},{3,19},{19,3},{4,20},{20... | collective-permute-start | bytes 73736 | tf_op jit(solution)/shard_map/ppermute | solution.py:513
  51.1 9.6 %collective-permute-start.10 = (f32[6,8,128]{2,1,0:T(8,128)S(1)}, f32[6,8,128]{2,1,0:T(8,128)S(1)}, u32[]{:S(2)}, u32[]{:S(2)}) collective-permute-start(f32[6,8,128]{2,1,0:T(8,128)S(1)} %get-tuple-element.42.ma), channel_id=1, source_target_pairs={{0,16},{16,0},{1,17},{17,1},{2,18},{18,2},{3,19},{19,3},{4,20},{20... | collective-permute-start | bytes 73736 | tf_op jit(solution)/shard_map/ppermute | solution.py:513
  53.2 3.7 %collective-permute-start.9 = (f32[4,8,128]{2,1,0:T(8,128)S(1)}, f32[4,8,128]{2,1,0:T(8,128)S(1)}, u32[]{:S(2)}, u32[]{:S(2)}) collective-permute-start(f32[4,8,128]{2,1,0:T(8,128)S(1)} %get-tuple-element.41.ma), channel_id=1, source_target_pairs={{0,16},{16,0},{1,17},{17,1},{2,18},{18,2},{3,19},{19,3},{4,20},{20... | collective-permute-start | bytes 49160 | tf_op jit(solution)/shard_map/ppermute | solution.py:513

commit v3 on v2

--- a/solution.py
+++ b/solution.py
@@ -272,7 +272,7 @@
     def get(j):
         return (side, outer[j]) if j in outer else (tiles, j)
 
-    @pl.loop(0, octants)
+    @pl.loop(0, octants, unroll=min(2, octants))
     def _(o):
         octant = first + o
         place = place_octant(octant)
@@ -315,7 +315,7 @@
             return below, j - layers - 1
         return (side, 2) if j == layers else (tiles, j)
 
-    @pl.loop(0, octants)
+    @pl.loop(0, octants, unroll=min(2, octants))
     def _(o):
         octant = first + o
         place = place_octant(octant)
@@ -342,7 +342,7 @@
         mom[j - 2] = jnp.zeros((8, LANES), F32)
     prepare(js, co, tab, keep)
 
-    @pl.loop(0, octants)
+    @pl.loop(0, octants, unroll=min(2, octants))
     def _(o):
         octant = first + o
         place = place_octant(octant)
@@ -375,7 +375,7 @@
     def get(j):
         return (edge, outer[j]) if j in outer else (new, j)
 
-    @pl.loop(0, octants)
+    @pl.loop(0, octants, unroll=min(2, octants))
     def _(o):
         octant = first + o
         place = place_octant(octant)
@@ -414,7 +414,7 @@
     def get1(j):
         return (rim, j + 4) if j < -2 else (edge, outer[j]) if j in outer else (new, j)
 
-    @pl.loop(0, octants)
+    @pl.loop(0, octants, unroll=min(2, octants))
     def _(o):
         octant = first + o
         place = place_octant(octant)
@@ -449,7 +449,7 @@
             return beside, outer[j]
         return (newer, slots[j]) if j in slots else (middle, j - 2)
 
-    @pl.loop(0, octants)
+    @pl.loop(0, octants, unroll=min(2, octants))
     def _(o):
         octant = first + o
         place = place_octant(octant)

time: 67.4 us -> 65.9 us (0.978)
  Pallas kernels: 30.9 us -> 29.5 us
    pallas_call x9, Pallas kernels: 30.9 us -> 29.5 us  [run(): return call(*args)]
  transfers between devices with their start and end apart: 11 -> 11, of which waited for: 3 -> 3; matrix products, arithmetic and copies ran while one was open for 0% -> 0% of each run, Pallas kernels for 35% -> 34%
where the time goes in v3:
time: 65.9 us; the launch traced here: 64.6 us
  Pallas kernels  29.5 us (45%)
  starting transfers between devices  25.6 us (39%)
  waiting for transfers between devices  9.32 us (14%)
    pallas_call x9, Pallas kernels, run(): return call(*args)  29.5 us
    ppermute x7, starting transfers between devices, send(): return lax.ppermute(block, ('oct', 'space'), pairs)  16.9 us
    ppermute x4, starting transfers between devices, exchange(): other = lax.ppermute(part, axis, [(i, i ^ bit) for i in range(count)])  8.7 us
    ppermute x4, waiting for transfers between devices, exchange(): other = lax.ppermute(part, axis, [(i, i ^ bit) for i in range(count)])  5.47 us
    ppermute x7, waiting for transfers between devices, send(): return lax.ppermute(block, ('oct', 'space'), pairs)  3.85 us
  transfers between devices with their start and end apart: 11, of which 3 were waited for; matrix products, arithmetic and copies ran while one was open for 0% of the time, Pallas kernels for 34%

profile of v3, /device:TPU:0, one launch (start us, length us, event | category | flops | bytes accessed | tf_op | source)
XLA Modules:
  0.0 64.6 jit_solution(4975189511400509786)
XLA Ops:
  0.0 0.1 pad_add_fusion.info
  0.1 2.5 %shard_map.37 = (f32[2,500,128]{2,1,0:T(8,128)}, f32[1,500,128]{2,1,0:T(8,128)}, f32[6,500,128]{2,1,0:T(8,128)S(1)}) custom-call(s32[2]{0:T(128)S(1)} %pad_add_fusion.info, f32[6,500,128]{2,1,0:T(8,128)} %bitcast.4), custom_call_target="tpu_custom_call" | custom-call | tf_op jit(solution)/shard_map/pallas_call | solution.py:502
  2.6 0.5 collective-permute-start
  3.2 2.6 %shard_map.38 = (f32[6,4,128,128]{3,2,1,0:T(8,128)S(1)}, f32[6,8,128]{2,1,0:T(8,128)S(1)}, f32[6,1,128]{2,1,0:T(1,128)S(1)}, f32[2,500,128]{2,1,0:T(8,128)}, f32...) custom-call(s32[2]{0:T(128)S(1)} %pad_add_fusion.info, f32[6,500,128]{2,1,0:T(8,128)S(1)} %get-tuple-element.24.x, ...), custom_call_target="tpu_custom_call" | custom-call | tf_op jit(solution)/shard_map/pallas_call | solution.py:502
  5.7 2.7 %collective-permute-start.4 = (f32[2,500,128]{2,1,0:T(8,128)}, f32[2,500,128]{2,1,0:T(8,128)S(1)}, u32[]{:S(2)}, u32[]{:S(2)}) collective-permute-start(f32[2,500,128]{2,1,0:T(8,128)} %get-tuple-element.34), channel_id=1, source_target_pairs={{0,1},{1,2},{2,3},{3,4},{4,5},{5,6},{6,7},{7,8},{8,9},{9,10},{10,1... | collective-permute-start | bytes 1536008 | tf_op jit(solution)/shard_map/ppermute | solution.py:536
  8.4 2.5 %collective-permute-start.5 = (f32[2,500,128]{2,1,0:T(8,128)}, f32[2,500,128]{2,1,0:T(8,128)S(1)}, u32[]{:S(2)}, u32[]{:S(2)}) collective-permute-start(f32[2,500,128]{2,1,0:T(8,128)} %get-tuple-element.35), channel_id=1, source_target_pairs={{1,0},{2,1},{3,2},{4,3},{5,4},{6,5},{7,6},{8,7},{9,8},{10,9},{11,1... | collective-permute-start | bytes 1536008 | tf_op jit(solution)/shard_map/ppermute | solution.py:536
  10.9 0.0 collective-permute-start.8
  10.9 6.5 %collective-permute-start.2 = (f32[6,8,128]{2,1,0:T(8,128)S(1)}, f32[6,8,128]{2,1,0:T(8,128)S(1)}, u32[]{:S(2)}, u32[]{:S(2)}) collective-permute-start(f32[6,8,128]{2,1,0:T(8,128)S(1)} %get-tuple-element.28.ma), channel_id=1, source_target_pairs={{0,16},{16,0},{1,17},{17,1},{2,18},{18,2},{3,19},{19,3},{4,20},{20... | collective-permute-start | bytes 73736 | tf_op jit(solution)/shard_map/ppermute | solution.py:513
  17.4 1.8 %collective-permute-done.2.mb = f32[6,8,128]{2,1,0:T(8,128)S(1)} collective-permute-done((f32[6,8,128]{2,1,0:T(8,128)S(1)}, f32[6,8,128]{2,1,0:T(8,128)S(1)}, u32[]{:S(2)}, u32[]{:S(2)}) %collective-permute-start.2) | collective-permute-done | bytes 24608 | tf_op jit(solution)/shard_map/ppermute | solution.py:513
  19.2 3.8 %collective-permute-done.1.l1 = f32[1,500,128]{2,1,0:T(8,128)S(1)} collective-permute-done((f32[1,500,128]{2,1,0:T(8,128)S(1)}, f32[1,500,128]{2,1,0:T(8,128)S(1)}, u32[]{:S(2)}, u32[]{:S(2)}) %collective-permute-start.1) | collective-permute-done | bytes 256032 | tf_op jit(solution)/shard_map/ppermute | solution.py:536
  23.0 4.7 %collective-permute-start.7 = (f32[6,8,128]{2,1,0:T(8,128)S(1)}, f32[6,8,128]{2,1,0:T(8,128)S(1)}, u32[]{:S(2)}, u32[]{:S(2)}) collective-permute-start(f32[6,8,128]{2,1,0:T(8,128)S(1)} %shard_map.41), channel_id=1, source_target_pairs={{1,0},{2,1},{3,2},{4,3},{5,4},{6,5},{7,6},{8,7},{9,8},{10,9},{11,1... | collective-permute-start | bytes 73736 | tf_op jit(solution)/shard_map/ppermute | solution.py:536
  27.8 0.0 collective-permute-done.h1
  27.8 6.5 %collective-permute-start.6 = (f32[6,8,128]{2,1,0:T(8,128)S(1)}, f32[6,8,128]{2,1,0:T(8,128)S(1)}, u32[]{:S(2)}, u32[]{:S(2)}) collective-permute-start(f32[6,8,128]{2,1,0:T(8,128)S(1)} %shard_map.41), channel_id=1, source_target_pairs={{0,1},{1,2},{2,3},{3,4},{4,5},{5,6},{6,7},{7,8},{8,9},{9,10},{10,1... | collective-permute-start | bytes 73736 | tf_op jit(solution)/shard_map/ppermute | solution.py:536
  34.3 5.1 %shard_map.39 = (f32[6,4,128,128]{3,2,1,0:T(8,128)S(1)}, f32[3,4,128,128]{3,2,1,0:T(8,128)S(1)}, f32[6,8,128]{2,1,0:T(8,128)S(1)}) custom-call(s32[2]{0:T(128)S(1)} %pad_add_fusion.info, f32[6,4,128,128]{3,2,1,0:T(8,128)S(1)} %get-tuple-element.25.tiles, f32[2,500,128]{2,1,0:T(8,128)S(1)} %collective-permute-done.h1, ...), custom_call_target="tpu_custom_call" | custom-call | tf_op jit(solution)/shard_map/pallas_call | solution.py:502
  39.4 0.0 collective-permute-done.7.down_share
  39.4 0.1 collective-permute-start.3
  39.5 4.1 %shard_map.42 = (f32[4,4,128,128]{3,2,1,0:T(8,128)S(1)}, f32[2,4,128,128]{3,2,1,0:T(8,128)S(1)}, f32[4,8,128]{2,1,0:T(8,128)S(1)}) custom-call(s32[2]{0:T(128)S(1)} %pad_add_fusion.info, f32[6,4,128,128]{3,2,1,0:T(8,128)S(1)} %get-tuple-element.25.tiles, f32[3,4,128,128]{3,2,1,0:T(8,128)S(1)} %get-tuple-element.33.side, ...), custom_call_target="tpu_custom_call" | custom-call | tf_op jit(solution)/shard_map/pallas_call | solution.py:502
  43.7 3.2 %shard_map.40 = (f32[3,4,128,128]{3,2,1,0:T(8,128)S(1)}, f32[3,8,128]{2,1,0:T(8,128)S(1)}) custom-call(s32[2]{0:T(128)S(1)} %pad_add_fusion.info, f32[6,4,128,128]{3,2,1,0:T(8,128)S(1)} %get-tuple-element.30.new, f32[6,8,128]{2,1,0:T(8,128)S(1)} %get-tuple-element.31.ma, f32[6,8,128]{2,1,0:T(8,128)S(1)} %collective-permute-done.3.mb, ...), custom_call_target="tpu_custom_call" | custom-call | tf_op jit(solution)/shard_map/pallas_call | solution.py:502
  46.9 3.3 %shard_map.43 = (f32[3,4,128,128]{3,2,1,0:T(8,128)S(1)}, f32[6,8,128]{2,1,0:T(8,128)S(1)}) custom-call(s32[2]{0:T(128)S(1)} %pad_add_fusion.info, f32[6,4,128,128]{3,2,1,0:T(8,128)S(1)} %get-tuple-element.30.new, f32[4,4,128,128]{3,2,1,0:T(8,128)S(1)} %get-tuple-element.36.edge, f32[6,8,128]{2,1,0:T(8,128)S(1)} %get-tuple-element.31.ma, ...), custom_call_target="tpu_custom_call" | custom-call | tf_op jit(solution)/shard_map/pallas_call | solution.py:502
  50.2 2.0 %collective-permute-start.10 = (f32[6,8,128]{2,1,0:T(8,128)S(1)}, f32[6,8,128]{2,1,0:T(8,128)S(1)}, u32[]{:S(2)}, u32[]{:S(2)}) collective-permute-start(f32[6,8,128]{2,1,0:T(8,128)S(1)} %get-tuple-element.42.ma), channel_id=1, source_target_pairs={{0,16},{16,0},{1,17},{17,1},{2,18},{18,2},{3,19},{19,3},{4,20},{20... | collective-permute-start | bytes 73736 | tf_op jit(solution)/shard_map/ppermute | solution.py:513
  52.2 0.1 collective-permute-start.9
  52.3 3.7 %collective-permute-done.9.mb = f32[4,8,128]{2,1,0:T(8,128)S(1)} collective-permute-done((f32[4,8,128]{2,1,0:T(8,128)S(1)}, f32[4,8,128]{2,1,0:T(8,128)S(1)}, u32[]{:S(2)}, u32[]{:S(2)}) %collective-permute-start.9) | collective-permute-done | bytes 16416 | tf_op jit(solution)/shard_map/ppermute | solution.py:513
  55.9 3.6 %shard_map.44.beside = f32[3,4,128,128]{3,2,1,0:T(8,128)S(1)} custom-call(s32[2]{0:T(128)S(1)} %pad_add_fusion.info, f32[3,4,128,128]{3,2,1,0:T(8,128)S(1)} %get-tuple-element.33.side, f32[2,4,128,128]{3,2,1,0:T(8,128)S(1)} %get-tuple-element.39.far, f32[2,500,128]{2,1,0:T(8,128)S(1)} %collective-permute-done.8.h3, ...), custom_call_target="tpu_custom_call" | custom-call | tf_op jit(solution)/shard_map/pallas_call | solution.py:502
  59.5 5.1 %shard_map.45 = f32[6,500,128]{2,1,0:T(8,128)} custom-call(s32[2]{0:T(128)S(1)} %pad_add_fusion.info, f32[3,4,128,128]{3,2,1,0:T(8,128)S(1)} %get-tuple-element.32.middle, f32[3,4,128,128]{3,2,1,0:T(8,128)S(1)} %get-tuple-element.38.newer, f32[3,4,128,128]{3,2,1,0:T(8,128)S(1)} %shard_map.44.beside, f32[6,8,128]{2,1,0:T(8,128)S(1)} %get-tuple-element.42.ma, ...), custom_call_target="tpu_custom_call" | custom-call | tf_op jit(solution)/shard_map/pallas_call | solution.py:502
  (15 shorter events, 0.0 us)
Async XLA Ops:
  0.0 3.2 %copy-start = (bf16[9,48,128]{2,1,0:T(8,128)(2,1)S(1)}, bf16[9,48,128]{2,1,0:T(8,128)(2,1)}, u32[]{:S(2)}) copy-start(bf16[9,48,128]{2,1,0:T(8,128)(2,1)} %constant.35.clone.tab.refs_0_) | copy-start | bytes 331780
  0.0 3.1 %copy-start.1 = (f32[1,6,128]{2,0,1:T(1,128)S(1)}, f32[1,6,128]{2,0,1:T(1,128)}, u32[]{:S(2)}) copy-start(f32[1,6,128]{2,0,1:T(1,128)} %param.4) | copy-start | bytes 9220
  2.6 16.6 %copy-start.2 = (f32[1,500,128]{2,1,0:T(8,128)S(1)}, f32[1,500,128]{2,1,0:T(8,128)}, u32[]{:S(2)}) copy-start(f32[1,500,128]{2,1,0:T(8,128)} %get-tuple-element.27) | copy-start | bytes 768004
  2.6 25.1 %collective-permute-start = (f32[2,500,128]{2,1,0:T(8,128)}, f32[2,500,128]{2,1,0:T(8,128)S(1)}, u32[]{:S(2)}, u32[]{:S(2)}) collective-permute-start(f32[2,500,128]{2,1,0:T(8,128)} %get-tuple-element.26), channel_id=1, source_target_pairs={{0,1},{1,2},{2,3},{3,4},{4,5},{5,6},{6,7},{7,8},{8,9},{9,10},{10,1... | collective-permute-start | bytes 1536008 | tf_op jit(solution)/shard_map/ppermute | solution.py:536
  5.7 33.7 %collective-permute-start.4 = (f32[2,500,128]{2,1,0:T(8,128)}, f32[2,500,128]{2,1,0:T(8,128)S(1)}, u32[]{:S(2)}, u32[]{:S(2)}) collective-permute-start(f32[2,500,128]{2,1,0:T(8,128)} %get-tuple-element.34), channel_id=1, source_target_pairs={{0,1},{1,2},{2,3},{3,4},{4,5},{5,6},{6,7},{7,8},{8,9},{9,10},{10,1... | collective-permute-start | bytes 1536008 | tf_op jit(solution)/shard_map/ppermute | solution.py:536
  8.4 31.1 %collective-permute-start.5 = (f32[2,500,128]{2,1,0:T(8,128)}, f32[2,500,128]{2,1,0:T(8,128)S(1)}, u32[]{:S(2)}, u32[]{:S(2)}) collective-permute-start(f32[2,500,128]{2,1,0:T(8,128)} %get-tuple-element.35), channel_id=1, source_target_pairs={{1,0},{2,1},{3,2},{4,3},{5,4},{6,5},{7,6},{8,7},{9,8},{10,9},{11,1... | collective-permute-start | bytes 1536008 | tf_op jit(solution)/shard_map/ppermute | solution.py:536
  10.9 41.4 %collective-permute-start.8 = (f32[2,500,128]{2,1,0:T(8,128)}, f32[2,500,128]{2,1,0:T(8,128)S(1)}, u32[]{:S(2)}, u32[]{:S(2)}) collective-permute-start(f32[2,500,128]{2,1,0:T(8,128)} %get-tuple-element.40), channel_id=1, source_target_pairs={{0,1},{1,2},{2,3},{3,4},{4,5},{5,6},{6,7},{7,8},{8,9},{9,10},{10,1... | collective-permute-start | bytes 1536008 | tf_op jit(solution)/shard_map/ppermute | solution.py:536
  10.9 8.3 %collective-permute-start.2 = (f32[6,8,128]{2,1,0:T(8,128)S(1)}, f32[6,8,128]{2,1,0:T(8,128)S(1)}, u32[]{:S(2)}, u32[]{:S(2)}) collective-permute-start(f32[6,8,128]{2,1,0:T(8,128)S(1)} %get-tuple-element.28.ma), channel_id=1, source_target_pairs={{0,16},{16,0},{1,17},{17,1},{2,18},{18,2},{3,19},{19,3},{4,20},{20... | collective-permute-start | bytes 73736 | tf_op jit(solution)/shard_map/ppermute | solution.py:513
  19.2 3.9 %collective-permute-start.1 = (f32[1,500,128]{2,1,0:T(8,128)S(1)}, f32[1,500,128]{2,1,0:T(8,128)S(1)}, u32[]{:S(2)}, u32[]{:S(2)}) collective-permute-start(f32[1,500,128]{2,1,0:T(8,128)S(1)} %copy-done.2), channel_id=1, source_target_pairs={{1,0},{2,1},{3,2},{4,3},{5,4},{6,5},{7,6},{8,7},{9,8},{10,9},{11,1... | collective-permute-start | bytes 768008 | tf_op jit(solution)/shard_map/ppermute | solution.py:536
  23.0 16.3 %collective-permute-start.7 = (f32[6,8,128]{2,1,0:T(8,128)S(1)}, f32[6,8,128]{2,1,0:T(8,128)S(1)}, u32[]{:S(2)}, u32[]{:S(2)}) collective-permute-start(f32[6,8,128]{2,1,0:T(8,128)S(1)} %shard_map.41), channel_id=1, source_target_pairs={{1,0},{2,1},{3,2},{4,3},{5,4},{6,5},{7,6},{8,7},{9,8},{10,9},{11,1... | collective-permute-start | bytes 73736 | tf_op jit(solution)/shard_map/ppermute | solution.py:536
  27.8 11.7 %collective-permute-start.6 = (f32[6,8,128]{2,1,0:T(8,128)S(1)}, f32[6,8,128]{2,1,0:T(8,128)S(1)}, u32[]{:S(2)}, u32[]{:S(2)}) collective-permute-start(f32[6,8,128]{2,1,0:T(8,128)S(1)} %shard_map.41), channel_id=1, source_target_pairs={{0,1},{1,2},{2,3},{3,4},{4,5},{5,6},{6,7},{7,8},{8,9},{9,10},{10,1... | collective-permute-start | bytes 73736 | tf_op jit(solution)/shard_map/ppermute | solution.py:536
  39.4 4.3 %collective-permute-start.3 = (f32[6,8,128]{2,1,0:T(8,128)S(1)}, f32[6,8,128]{2,1,0:T(8,128)S(1)}, u32[]{:S(2)}, u32[]{:S(2)}) collective-permute-start(f32[6,8,128]{2,1,0:T(8,128)S(1)} %get-tuple-element.31.ma), channel_id=1, source_target_pairs={{0,16},{16,0},{1,17},{17,1},{2,18},{18,2},{3,19},{19,3},{4,20},{20... | collective-permute-start | bytes 73736 | tf_op jit(solution)/shard_map/ppermute | solution.py:513
  50.2 9.4 %collective-permute-start.10 = (f32[6,8,128]{2,1,0:T(8,128)S(1)}, f32[6,8,128]{2,1,0:T(8,128)S(1)}, u32[]{:S(2)}, u32[]{:S(2)}) collective-permute-start(f32[6,8,128]{2,1,0:T(8,128)S(1)} %get-tuple-element.42.ma), channel_id=1, source_target_pairs={{0,16},{16,0},{1,17},{17,1},{2,18},{18,2},{3,19},{19,3},{4,20},{20... | collective-permute-start | bytes 73736 | tf_op jit(solution)/shard_map/ppermute | solution.py:513
  52.2 3.7 %collective-permute-start.9 = (f32[4,8,128]{2,1,0:T(8,128)S(1)}, f32[4,8,128]{2,1,0:T(8,128)S(1)}, u32[]{:S(2)}, u32[]{:S(2)}) collective-permute-start(f32[4,8,128]{2,1,0:T(8,128)S(1)} %get-tuple-element.41.ma), channel_id=1, source_target_pairs={{0,16},{16,0},{1,17},{17,1},{2,18},{18,2},{3,19},{19,3},{4,20},{20... | collective-permute-start | bytes 49160 | tf_op jit(solution)/shard_map/ppermute | solution.py:513
